TPU v7x, 32 devices: a whole 2x2x4 slice. The times are simulated.
32 devices in a mesh: gx: 16 (over z, y, x), gy: 2 (over core).
Axes of the slice: x: 2, y: 2, z: 4, core: 2. Of those that a mesh axis runs over, the one named last changes fastest.
Arguments:
- spectra: bfloat16 [2, 2, 512, 256], P(None, None, 'gx', 'gy'), may hold values from -1 to 7, as said below
- noise_weights: bfloat16 [2, 2, 512, 256], P(None, None, 'gx', 'gy'), may hold values from 0.049804688 to 1
- mixing: float32 [2, 2], replicated, may hold values from 0.2 to 2, as said below
Outputs:
- material: float32 [2, 2, 512, 256], P(None, None, 'gx', 'gy')
Inputs may be any that keep to these rules, and one draw needn't show every extreme that they name: `spectra`: smooth water and bone structure with sharp bone edges, plus voxel noise. `mixing`: diagonal entries lie between 1 and 2, the others between 0.2 and 0.6.
All inputs are finite; a program needn't handle non-finite values.
Results may differ from a plain program's by a relative error of at most 0.0003.
Values sent between devices are 32-bit elements; how exact they have to be, the bound alone decides.
No kernel may reach another device: no remote copies, remote signals or barrier semaphores. Data moves between devices by JAX's collectives and lax.ppermute only.
A program may use at most 64 MiB of HBM per device.

v0:
```python
import jax
import jax.numpy as jnp
from jax import lax
from jax.experimental import pallas as pl
from jax.experimental.pallas import tpu as pltpu
from jax.sharding import PartitionSpec as P

LEVELS = 6
COARSE_SWEEPS = 4
JOIN = 3

huber_delta = 0.05
relaxation = 0.8
smoothness = 256.0

LANES = 128
SUB = 8


def penalty_of(level):
    return smoothness / 4.0**level


def lane_of(shape=(SUB, LANES)):
    return lax.broadcasted_iota(jnp.int32, shape, 1)


def row_of(shape=(SUB, LANES)):
    return lax.broadcasted_iota(jnp.int32, shape, 0)


def roll_lanes(x, shift):
    return pltpu.roll(x, shift % LANES, axis=1)


def roll_rows(x, shift):
    return pltpu.roll(x, shift % x.shape[0], axis=0)


def take_lanes(x, index):
    return jnp.take_along_axis(x, index, axis=1)


def from_right(tiles, step=1):
    rolled = [roll_lanes(tile, -step) for tile in tiles]
    if len(tiles) == 1:
        return rolled
    inside = lane_of(tiles[0].shape) < LANES - step
    return [
        jnp.where(inside, rolled[k], rolled[(k + 1) % len(tiles)]) for k in range(len(tiles))
    ]


def from_left(tiles, step=1):
    rolled = [roll_lanes(tile, step) for tile in tiles]
    if len(tiles) == 1:
        return rolled
    inside = lane_of(tiles[0].shape) >= step
    return [jnp.where(inside, rolled[k], rolled[k - 1]) for k in range(len(tiles))]


def flux(gap, with_factor):
    if not with_factor:
        return jnp.clip(gap, -huber_delta, huber_delta), None
    factor = huber_delta / jnp.maximum(jnp.abs(gap), huber_delta)
    return factor * gap, factor


def keep(mask, value):
    return value if mask is None or value is None else jnp.where(mask, value, 0.0)


def row_sums(tiles, masks, with_factor, step=1):
    right = from_right(tiles, step)
    flows, factors = [], []
    for k, tile in enumerate(tiles):
        flow, factor = flux(right[k] - tile, with_factor)
        flows.append(keep(masks[k], flow))
        factors.append(keep(masks[k], factor))
    back = from_left(flows, step)
    flow_sum = [flows[k] - back[k] for k in range(len(tiles))]
    if not with_factor:
        return flow_sum, None
    back = from_left(factors, step)
    return flow_sum, [factors[k] + back[k] for k in range(len(tiles))]


def row_sums_split(tiles, masks, with_factor):
    half = len(tiles) // 2
    even, odd = tiles[:half], tiles[half:]
    after = from_right(even)
    inner = [flux(odd[k] - even[k], with_factor) for k in range(half)]
    outer = [flux(after[k] - odd[k], with_factor) for k in range(half)]
    outer = [tuple(keep(masks[k], part) for part in outer[k]) for k in range(half)]
    back = from_left([part[0] for part in outer])
    flow_sum = [inner[k][0] - back[k] for k in range(half)]
    flow_sum += [outer[k][0] - inner[k][0] for k in range(half)]
    if not with_factor:
        return flow_sum, None
    back = from_left([part[1] for part in outer])
    factor_sum = [inner[k][1] + back[k] for k in range(half)]
    factor_sum += [inner[k][1] + outer[k][1] for k in range(half)]
    return flow_sum, factor_sum


def column_masks(tiles, width, step=1):
    masks = []
    for k in range(tiles):
        place = (lane_of() + k * LANES) % width
        ends = any((k * LANES + n) % width >= width - step for n in range(LANES))
        masks.append(place < width - step if ends else None)
    return masks


class Grid:
    def __init__(self, level, sizes):
        self.level = level
        self.penalty = penalty_of(level)
        self.own = sizes.rows >> level
        self.rows = 3 * self.own
        self.split = level == 0
        self.masks = None
        if level == 0:
            self.groups, self.tiles = sizes.slices, 2 * sizes.tiles
            self.mask_place = (sizes.tiles, sizes.tiles * LANES)
        elif level == 1:
            self.groups, self.tiles = sizes.slices, sizes.tiles
            self.mask_place = (self.tiles, sizes.tiles * LANES)
        else:
            self.groups, self.tiles = 1, sizes.slices * sizes.tiles // 2
            self.mask_place = (self.tiles, sizes.tiles * LANES // 2)

    def shape(self, members):
        return (self.groups, members, self.tiles, self.rows + SUB, LANES)

    def across(self, tiles, with_factor):
        if self.masks is None:
            self.masks = column_masks(*self.mask_place)
        if self.split:
            return row_sums_split(tiles, self.masks, with_factor)
        return row_sums(tiles, self.masks, with_factor)

    def row_mask(self, start, ends):
        mask = None
        for edge, inside in zip((self.own - 1, 2 * self.own - 1), ends):
            if start <= edge < start + SUB:
                part = jnp.logical_or(row_of() != edge - start, inside)
                mask = part if mask is None else jnp.logical_and(mask, part)
        return mask


class Sizes:
    def __init__(self, slices, rows, columns, row_devices, column_devices):
        self.slices = slices
        self.rows = rows
        self.row_devices = row_devices
        self.column_devices = column_devices
        self.columns = columns
        self.tiles = column_devices * columns // (2 * LANES)
        self.join_rows = rows >> JOIN
        self.join_tiles = slices * self.tiles // 2
        self.join_width = self.tiles * LANES >> (JOIN - 1)
        self.grids = [Grid(level, self) for level in range(JOIN)]


def sweep(grid, ends, field, first, last, with_factor, emit):
    strips = range(first, last)
    for group in range(grid.groups):

        def vertical(start, member, tile, center):
            below = field[group, member, tile, pl.ds(start + 1, SUB), :]
            flow, factor = flux(below - center, with_factor)
            mask = grid.row_mask(start, ends)
            return keep(mask, flow), keep(mask, factor)

        carry = {}
        for member in range(2):
            for tile in range(grid.tiles):
                if first > 0:
                    start = (first - 1) * SUB
                    center = field[group, member, tile, pl.ds(start, SUB), :]
                    parts = vertical(start, member, tile, center)
                    carry[member, tile] = [None if x is None else roll_rows(x, 1) for x in parts]
                else:
                    zero = jnp.zeros((SUB, LANES), jnp.float32)
                    carry[member, tile] = [zero, zero]
        top = row_of() == 0
        for strip in strips:
            start = strip * SUB
            centers, flows, factors = [], [], []
            for member in range(2):
                tiles = [
                    field[group, member, tile, pl.ds(start, SUB), :] for tile in range(grid.tiles)
                ]
                flow_sum, factor_sum = grid.across(tiles, with_factor)
                for tile in range(grid.tiles):
                    flow, factor = vertical(start, member, tile, tiles[tile])
                    rolled = roll_rows(flow, 1)
                    above = jnp.where(top, carry[member, tile][0], rolled)
                    flow_sum[tile] = flow_sum[tile] + (flow - above)
                    carry[member, tile][0] = rolled
                    if with_factor:
                        rolled = roll_rows(factor, 1)
                        above = jnp.where(top, carry[member, tile][1], rolled)
                        factor_sum[tile] = factor_sum[tile] + (factor + above)
                        carry[member, tile][1] = rolled
                centers.append(tiles)
                flows.append(flow_sum)
                factors.append(factor_sum)
            emit(group, start, centers, flows, factors)


def solve_pair(water, cross, bone, right_water, right_bone):
    scale = relaxation / (water * bone - cross * cross)
    return (
        scale * (bone * right_water - cross * right_bone),
        scale * (water * right_bone - cross * right_water),
    )


def relax_strips(grid, ends, field, source, data, first, last):
    p = grid.penalty

    def emit(group, start, centers, flows, factors):
        rows = pl.ds(start, SUB)
        for tile in range(grid.tiles):
            water, cross, bone = (data[group, m, tile, rows, :] for m in range(3))
            u, v = centers[0][tile], centers[1][tile]
            right = [
                source[group, 0, tile, rows, :] - (water * u + cross * v) + p * flows[0][tile],
                source[group, 1, tile, rows, :] - (cross * u + bone * v) + p * flows[1][tile],
            ]
            du, dv = solve_pair(
                water + p * factors[0][tile], cross, bone + p * factors[1][tile], *right
            )
            field[group, 0, tile, rows, :] = u + du
            field[group, 1, tile, rows, :] = v + dv

    sweep(grid, ends, field, first, last, True, emit)


def first_relax_strips(grid, ends, field, source, data, first, last):
    p = grid.penalty

    def emit(group, start, centers, flows, factors):
        rows = pl.ds(start, SUB)
        for tile in range(grid.tiles):
            water, cross, bone = (data[group, m, tile, rows, :] for m in range(3))
            u, v = centers[0][tile], centers[1][tile]
            right = [source[group, m, tile, rows, :] for m in range(2)]
            source[group, 0, tile, rows, :] = right[0] + (
                (water * u + cross * v) - p * flows[0][tile]
            )
            source[group, 1, tile, rows, :] = right[1] + (
                (cross * u + bone * v) - p * flows[1][tile]
            )
            du, dv = solve_pair(
                water + p * factors[0][tile], cross, bone + p * factors[1][tile], *right
            )
            field[group, 0, tile, rows, :] = u + du
            field[group, 1, tile, rows, :] = v + dv

    sweep(grid, ends, field, first, last, True, emit)


def residual_strips(grid, ends, field, source, data, out, first, last):
    p = grid.penalty

    def emit(group, start, centers, flows, factors):
        rows = pl.ds(start, SUB)
        rests = [[], []]
        for tile in range(grid.tiles):
            water, cross, bone = (data[group, m, tile, rows, :] for m in range(3))
            u, v = centers[0][tile], centers[1][tile]
            rests[0].append(
                source[group, 0, tile, rows, :] - (water * u + cross * v) + p * flows[0][tile]
            )
            rests[1].append(
                source[group, 1, tile, rows, :] - (cross * u + bone * v) + p * flows[1][tile]
            )
        for member in range(2):
            parts = rests[member]
            if grid.split:
                half = grid.tiles // 2
                parts = [parts[k] + parts[half + k] for k in range(half)]
            for tile, part in enumerate(parts):
                out[group, member, tile, rows, :] = part

    sweep(grid, ends, field, first, last, False, emit)


def pair_rows(ref, group, member, tile, start):
    upper = ref[group, member, tile, pl.ds(2 * start, SUB, stride=2), :]
    lower = ref[group, member, tile, pl.ds(2 * start + 1, SUB, stride=2), :]
    return upper + lower


def merge_pair(first, second):
    index = (2 * lane_of()) % LANES
    halves = [take_lanes(x + roll_lanes(x, -1), index) for x in (first, second)]
    return jnp.where(lane_of() < LANES // 2, halves[0], halves[1])


def split_pair(value):
    index = lane_of() // 2
    return take_lanes(value, index), take_lanes(value, index + LANES // 2)


def restrict_first(grids, ref, out, members, first, last, summed=False):
    coarse = grids[1]
    for group in range(coarse.groups):
        for member in range(members):
            for tile in range(coarse.tiles):
                for strip in range(first, last):
                    start = strip * SUB
                    total = pair_rows(ref, group, member, tile, start)
                    if not summed:
                        total = total + pair_rows(ref, group, member, coarse.tiles + tile, start)
                    for target in out:
                        target[group, member, tile, pl.ds(start, SUB), :] = 0.25 * total


def restrict_second(grids, ref, out, members, first, last):
    fine, coarse = grids[1], grids[2]
    places = [(group, tile) for group in range(fine.groups) for tile in range(fine.tiles)]
    for member in range(members):
        for tile in range(coarse.tiles):
            for strip in range(first, last):
                start = strip * SUB
                pair = [
                    pair_rows(ref, g, member, t, start) for g, t in places[2 * tile : 2 * tile + 2]
                ]
                merged = 0.25 * merge_pair(*pair)
                for target in out:
                    target[0, member, tile, pl.ds(start, SUB), :] = merged


def join_tiles(grids, ref, members):
    grid = grids[2]
    flat = [
        pair_rows(ref, 0, member, tile, grid.own // 2)
        for member in members
        for tile in range(grid.tiles)
    ]
    return [0.25 * merge_pair(flat[2 * k], flat[2 * k + 1]) for k in range(len(flat) // 2)]


def descend(sizes, ends, state, message_fields, message, first_rows):
    grids = sizes.grids
    u, f, d, uc, rest = state
    (a0, z0), (a1, z1) = first_rows
    residual_strips(grids[0], ends, u[0], f[0], d[0], rest[0], a0, z0)
    restrict_first(grids, u[0], (u[1], uc[1]), 2, a1, z1)
    restrict_first(grids, rest[0], (f[1],), 2, a1, z1, summed=True)
    first_relax_strips(grids[1], ends, u[1], f[1], d[1], a1, z1)
    residual_strips(grids[1], ends, u[1], f[1], d[1], rest[1], a1, z1)
    strips = grids[2].rows // SUB
    restrict_second(grids, u[1], (u[2], uc[2]), 2, 0, strips)
    restrict_second(grids, rest[1], (f[2],), 2, 0, strips)
    first_relax_strips(grids[2], ends, u[2], f[2], d[2], 0, strips)
    residual_strips(grids[2], ends, u[2], f[2], d[2], rest[2], 0, strips)
    h = sizes.join_rows
    fields = [join_tiles(grids, u[2], (0, 1)), join_tiles(grids, rest[2], (0, 1))]
    if message_fields == 4:
        fields += [join_tiles(grids, d[2], (0, 2)), join_tiles(grids, d[2], (1, 1))]
    for place, tiles in enumerate(fields):
        for k, tile in enumerate(tiles):
            for target in range(sizes.row_devices):
                message[target, k, pl.ds(place * h, h), :] = tile[:h]


def coarse_correction(sizes, fields):
    tiles = sizes.join_tiles
    rows = sizes.row_devices * sizes.join_rows
    width = sizes.join_width
    shape = (rows, LANES)
    row, lane = row_of(shape), lane_of(shape)

    def partner(values):
        if len(values) == 1:
            return [roll_lanes(values[0], LANES // 2)]
        half = len(values) // 2
        return values[half:] + values[:half]

    def mean(values, step):
        pair = (lane & step) == 0
        right, left = from_right(values, step), from_left(values, step)
        values = [x + jnp.where(pair, r, s) for x, r, s in zip(values, right, left)]
        pair = (row & step) == 0
        return [
            0.25 * (x + jnp.where(pair, roll_rows(x, -step), roll_rows(x, step))) for x in values
        ]

    estimate, rest, diagonal, cross = fields
    diagonals, crosses = [diagonal], [cross]
    for level in range(JOIN + 1, LEVELS):
        step = 1 << (level - JOIN - 1)
        diagonals.append(mean(diagonals[-1], step))
        crosses.append(mean(crosses[-1], step))

    def sums(level, values, with_factor):
        step = 1 << (level - JOIN)
        masks = [(lane + k * LANES) % width < width - step for k in range(tiles)]
        flow_sum, factor_sum = row_sums(values, masks, with_factor, step)
        below = row < rows - step
        for k, value in enumerate(values):
            flow, factor = flux(roll_rows(value, -step) - value, with_factor)
            flow = keep(below, flow)
            flow_sum[k] = flow_sum[k] + (flow - roll_rows(flow, step))
            if with_factor:
                factor = keep(below, factor)
                factor_sum[k] = factor_sum[k] + (factor + roll_rows(factor, step))
        return flow_sum, factor_sum

    def apply(level, values, flow_sum):
        p = penalty_of(level)
        other = partner(values)
        d, x = diagonals[level - JOIN], crosses[level - JOIN]
        return [
            d[k] * values[k] + x[k] * other[k] - p * flow_sum[k] for k in range(tiles)
        ]

    def solve(level, values, factor_sum, right):
        p = penalty_of(level)
        d, x = diagonals[level - JOIN], crosses[level - JOIN]
        h = [d[k] + p * factor_sum[k] for k in range(tiles)]
        h_other, r_other = partner(h), partner(right)
        return [
            values[k]
            + relaxation
            / (h[k] * h_other[k] - x[k] * x[k])
            * (h_other[k] * right[k] - x[k] * r_other[k])
            for k in range(tiles)
        ]

    def relax(level, values, source):
        flow_sum, factor_sum = sums(level, values, True)
        image = apply(level, values, flow_sum)
        return solve(level, values, factor_sum, [a - b for a, b in zip(source, image)])

    def cycle(level, values, rest):
        flow_sum, factor_sum = sums(level, values, True)
        image = apply(level, values, flow_sum)
        source = [a + b for a, b in zip(rest, image)]
        start = values
        values = solve(level, values, factor_sum, rest)
        if level == LEVELS - 1:
            for _ in range(COARSE_SWEEPS - 1):
                values = relax(level, values, source)
        else:
            step = 1 << (level - JOIN)
            image = apply(level, values, sums(level, values, False)[0])
            coarse_rest = mean([a - b for a, b in zip(source, image)], step)
            correction = cycle(level + 1, mean(values, step), coarse_rest)
            values = relax(level, [a + b for a, b in zip(values, correction)], source)
        return [a - b for a, b in zip(values, start)]

    return cycle(JOIN, estimate, rest)


def ascend(sizes, ends, row_index, received, state, scratch, level_rows):
    grids = sizes.grids
    u, f, d, uc = state
    gathered, correction, raised = scratch
    h = sizes.join_rows
    whole = sizes.row_devices * h
    fields = []
    for place, (ref, field) in enumerate(received):
        tiles = []
        for k in range(sizes.join_tiles):
            for source in range(sizes.row_devices):
                gathered[place, k, pl.ds(source * h, h), :] = ref[source, k, pl.ds(field * h, h), :]
            tiles.append(gathered[place, k])
        fields.append(tiles)
    values = coarse_correction(sizes, fields)
    for k in range(sizes.join_tiles):
        correction[k, :SUB, :] = jnp.zeros((SUB, LANES), jnp.float32)
        correction[k, pl.ds(SUB, whole), :] = values[k]
        correction[k, pl.ds(SUB + whole, 2 * SUB), :] = jnp.zeros((2 * SUB, LANES), jnp.float32)

    grid = grids[2]
    strips = grid.rows // SUB
    base = row_index * h + SUB - h
    for k in range(sizes.join_tiles):
        for start in range(0, 3 * h, SUB):
            parts = split_pair(correction[k, pl.ds(base + start, SUB), :])
            for side, part in enumerate(parts):
                member, tile = divmod(2 * k + side, grid.tiles)
                for odd in range(2):
                    raised[2][0, member, tile, pl.ds(2 * start + odd, SUB, stride=2), :] = part
    add_raised(grid, u[2], raised[2], 0, strips)
    relax_strips(grid, ends, u[2], f[2], d[2], 0, strips)

    fine = grids[1]
    places = [(group, tile) for group in range(fine.groups) for tile in range(fine.tiles)]
    for member in range(2):
        for tile in range(grid.tiles):
            for strip in range(strips):
                start = strip * SUB
                rows = pl.ds(start, SUB)
                parts = split_pair(u[2][0, member, tile, rows, :] - uc[2][0, member, tile, rows, :])
                for (g, t), part in zip(places[2 * tile : 2 * tile + 2], parts):
                    for odd in range(2):
                        raised[1][g, member, t, pl.ds(2 * start + odd, SUB, stride=2), :] = part
    (a0, z0), (a1, z1) = level_rows
    add_raised(fine, u[1], raised[1], 0, fine.rows // SUB)
    relax_strips(fine, ends, u[1], f[1], d[1], a1, z1)

    for group in range(fine.groups):
        for member in range(2):
            for tile in range(fine.tiles):
                for strip in range(a1, z1):
                    start = strip * SUB
                    rows = pl.ds(start, SUB)
                    part = u[1][group, member, tile, rows, :] - uc[1][group, member, tile, rows, :]
                    for odd in range(2):
                        raised[0][group, member, tile, pl.ds(2 * start + odd, SUB, stride=2), :] = part
    add_raised(grids[0], u[0], raised[0], 2 * a1, 2 * z1)
    relax_strips(grids[0], ends, u[0], f[0], d[0], a0, z0)


def add_raised(grid, field, raised, first, last):
    period = grid.tiles // 2 if grid.split else grid.tiles
    for group in range(grid.groups):
        for member in range(2):
            for tile in range(grid.tiles):
                for strip in range(first, last):
                    rows = pl.ds(strip * SUB, SUB)
                    field[group, member, tile, rows, :] = (
                        field[group, member, tile, rows, :]
                        + raised[group, member, tile % period, rows, :]
                    )


def zero_margin(grid, ref):
    for group in range(grid.groups):
        for member in range(2):
            for tile in range(grid.tiles):
                ref[group, member, tile, pl.ds(grid.rows, SUB), :] = jnp.zeros(
                    (SUB, LANES), jnp.float32
                )


def domain_ends(sizes):
    row_index = lax.axis_index("gx")
    return row_index, (row_index > 0, row_index < sizes.row_devices - 1)


def start_kernel(sizes, mixing, raw, u0, u1, u2, f0, f1, f2, d0, d1, d2, uc1, uc2, message, *rest):
    grids = sizes.grids
    row_index, ends = domain_ends(sizes)
    for grid, ref in zip(grids, (u0, u1, u2)):
        zero_margin(grid, ref)
    m = [[mixing[i, j] for j in range(2)] for i in range(2)]
    water = [m[0][0] * m[0][0], m[1][0] * m[1][0]]
    cross = [m[0][0] * m[0][1], m[1][0] * m[1][1]]
    bone = [m[0][1] * m[0][1], m[1][1] * m[1][1]]
    odd_device = row_index % 2
    parts = (2 - odd_device, 0, 1 + odd_device)
    beyond = (
        jnp.where(ends[0], 0.0, 1.0),
        None,
        jnp.where(ends[1], 0.0, 1.0),
    )
    grid = grids[0]
    lane, row = lane_of(), row_of()
    low = lane < LANES // 2
    even_first = jnp.where(low, 2 * lane, 2 * lane - LANES + 1)
    odd_first = jnp.where(low, 2 * lane + 1, 2 * lane - LANES)
    half = sizes.tiles
    p = grid.penalty
    for group in range(grid.groups):
        for strip in range(grid.rows // SUB):
            start = strip * SUB
            part, inner = divmod(start, sizes.rows)

            def load(kind, energy, tile):
                plane = (2 * kind + energy) * sizes.slices + group
                pieces = [
                    raw[2 * tile + side, parts[part], plane, pl.ds(inner, SUB), :]
                    for side in range(2)
                ]
                if kind == 1 and beyond[part] is not None:
                    pieces = [piece + beyond[part] for piece in pieces]
                first = take_lanes(pieces[0], even_first)
                second = take_lanes(pieces[1], odd_first)
                return (
                    jnp.where(low, first, second),
                    roll_lanes(jnp.where(low, second, first), LANES // 2),
                )

            vertical = jnp.full((SUB, LANES), 2.0, jnp.float32)
            for edge, inside in zip((grid.own - 1, 2 * grid.own - 1), ends):
                for place in (edge, edge + 1):
                    if start <= place < start + SUB:
                        missing = jnp.logical_and(row == place - start, jnp.logical_not(inside))
                        vertical = jnp.where(missing, vertical - 1.0, vertical)
            for tile in range(half):
                counts = [load(0, energy, tile) for energy in range(2)]
                weights = [load(1, energy, tile) for energy in range(2)]
                for parity in range(2):
                    y = [counts[energy][parity] for energy in range(2)]
                    w = [weights[energy][parity] for energy in range(2)]
                    dw = w[0] * water[0] + w[1] * water[1]
                    dx = w[0] * cross[0] + w[1] * cross[1]
                    db = w[0] * bone[0] + w[1] * bone[1]
                    t = [w[energy] * y[energy] for energy in range(2)]
                    fw = t[0] * m[0][0] + t[1] * m[1][0]
                    fb = t[0] * m[0][1] + t[1] * m[1][1]
                    total = vertical + 2.0
                    if parity == 0 and tile == 0:
                        total = jnp.where(lane == 0, total - 1.0, total)
                    if parity == 1 and tile == half - 1:
                        total = jnp.where(lane == LANES - 1, total - 1.0, total)
                    total = p * total
                    uw, ub = solve_pair(dw + total, dx, db + total, fw, fb)
                    k = parity * half + tile
                    rows = pl.ds(start, SUB)
                    for member, value in enumerate((dw, dx, db)):
                        d0[group, member, k, rows, :] = value
                    for member, value in enumerate((fw, fb)):
                        f0[group, member, k, rows, :] = value
                    for member, value in enumerate((uw, ub)):
                        u0[group, member, k, rows, :] = value
    restrict_first(grids, d0, (d1,), 3, 0, grids[1].rows // SUB)
    restrict_second(grids, d1, (d2,), 3, 0, grids[2].rows // SUB)
    state = ((u0, u1, u2), (f0, f1, f2), (d0, d1, d2), (None, uc1, uc2), rest)
    all_rows = ((0, grids[0].rows // SUB), (0, grids[1].rows // SUB))
    descend(sizes, ends, state, 4, message, all_rows)


def middle_rows(sizes):
    return (
        (sizes.rows // 2 // SUB, 5 * sizes.rows // 2 // SUB),
        (sizes.rows // 4 // SUB, 5 * sizes.rows // 4 // SUB),
    )


def middle_kernel(
    sizes, received, u0i, u1i, u2i, f0, f1i, f2i, d0, d1, d2, uc1i, uc2i,
    u0, u1, u2, f1, f2, uc1, uc2, message,
    gathered, correction, raised0, raised1, raised2, *rest,
):
    grids = sizes.grids
    row_index, ends = domain_ends(sizes)
    for source, target in ((u0i, u0), (u1i, u1), (u2i, u2)):
        target[...] = source[...]
    scratch = (gathered, correction, (raised0, raised1, raised2))
    fields = [(received, k) for k in range(4)]
    span = middle_rows(sizes)
    state = ((u0, u1, u2), (f0, f1i, f2i), (d0, d1, d2), (None, uc1i, uc2i))
    ascend(sizes, ends, row_index, fields, state, scratch, span)
    (a0, z0), _ = span
    relax_strips(grids[0], ends, u0, f0, d0, a0, z0)
    zero_margin(grids[1], u1)
    zero_margin(grids[2], u2)
    state = ((u0, u1, u2), (f0, f1, f2), (d0, d1, d2), (None, uc1, uc2), rest)
    descend(sizes, ends, state, 2, message, span)


def last_kernel(
    sizes, received, first_received, u0, u1, u2, f0, f1, f2, d0, d1, d2, uc1, uc2,
    out,
    v0, v1, v2, gathered, correction, raised0, raised1, raised2,
):
    grids = sizes.grids
    row_index, ends = domain_ends(sizes)
    for source, target in ((u0, v0), (u1, v1), (u2, v2)):
        target[...] = source[...]
    scratch = (gathered, correction, (raised0, raised1, raised2))
    fields = [(received, 0), (received, 1), (first_received, 2), (first_received, 3)]
    own = (sizes.rows // SUB, 2 * sizes.rows // SUB)
    span = (own, middle_rows(sizes)[1])
    state = ((v0, v1, v2), (f0, f1, f2), (d0, d1, d2), (None, uc1, uc2))
    ascend(sizes, ends, row_index, fields, state, scratch, span)
    column_index = lax.axis_index("gy")
    lane = lane_of()
    tile = column_index // 2
    index = (column_index % 2) * (LANES // 2) + lane // 2
    even = lane % 2 == 0
    for group in range(grids[0].groups):
        for member in range(2):
            for strip in range(*own):
                rows = pl.ds(strip * SUB, SUB)
                first = v0[group, member, tile, rows, :]
                second = v0[group, member, tile + sizes.tiles, rows, :]
                out[member, group, pl.ds(strip * SUB - sizes.rows, SUB), :] = jnp.where(
                    even, take_lanes(first, index), take_lanes(second, index)
                )


def shaped(shape):
    return jax.ShapeDtypeStruct(shape, jnp.float32)


def local(spectra, noise_weights, mixing):
    row_devices, column_devices = lax.axis_size("gx"), lax.axis_size("gy")
    _, slices, rows, columns = spectra.shape
    extents = (slices, rows, columns, row_devices, column_devices)
    sizes = Sizes(*extents)
    grids = sizes.grids
    flat = (2 * slices, rows, columns)
    raw = jnp.concatenate(
        [
            spectra.astype(jnp.float32).reshape(flat),
            noise_weights.astype(jnp.float32).reshape(flat),
        ]
    )
    near, far = [], []
    for i in range(row_devices - 1):
        (far if i % 2 else near).extend([(i, i + 1), (i + 1, i)])
    beside = [lax.ppermute(raw, "gx", far), lax.ppermute(raw, "gx", near)][::-1]
    whole = lax.all_gather(jnp.stack([raw] + beside), "gy")

    def vmem(shape):
        return pltpu.VMEM(shape, jnp.float32)

    def message_shape(fields):
        return (row_devices, sizes.join_tiles, fields * sizes.join_rows, LANES)

    fields = [grid.shape(2) for grid in grids]
    datas = [grid.shape(3) for grid in grids]

    def halved(shape):
        return shape[:2] + (shape[2] // 2,) + shape[3:]

    rests = [vmem(halved(fields[0])), vmem(fields[1]), vmem(fields[2])]
    join_whole = row_devices * sizes.join_rows
    coarse = [
        vmem((4, sizes.join_tiles, join_whole, LANES)),
        vmem((sizes.join_tiles, join_whole + 3 * SUB, LANES)),
        vmem(halved(fields[0])),
        vmem(fields[1]),
        vmem(fields[2]),
    ]

    def call(body, outs, scratch, in_specs=None):
        kernel = lambda *refs: body(Sizes(*extents), *refs)
        extra = {} if in_specs is None else {"in_specs": in_specs}
        return pl.pallas_call(
            kernel,
            out_shape=[shaped(shape) for shape in outs],
            scratch_shapes=scratch,
            name=body.__name__,
            **extra,
        )

    outs = fields + fields + datas + fields[1:] + [message_shape(4)]
    specs = [pl.BlockSpec(memory_space=pltpu.SMEM), pl.BlockSpec(memory_space=pltpu.VMEM)]
    u0, u1, u2, f0, f1, f2, d0, d1, d2, uc1, uc2, message = call(
        start_kernel, outs, rests, specs
    )(mixing, whole)
    first_received = lax.all_to_all(message, "gx", 0, 0, tiled=True)
    outs = fields + fields[1:] + fields[1:] + [message_shape(2)]
    u0, u1, u2, f1, f2, uc1, uc2, message = call(middle_kernel, outs, coarse + rests)(
        first_received, u0, u1, u2, f0, f1, f2, d0, d1, d2, uc1, uc2
    )
    received = lax.all_to_all(message, "gx", 0, 0, tiled=True)
    outs = [(2, slices, rows, columns)]
    return call(last_kernel, outs, [vmem(shape) for shape in fields] + coarse)(
        received, first_received, u0, u1, u2, f0, f1, f2, d0, d1, d2, uc1, uc2
    )[0]


def solution(mesh):
    return jax.shard_map(
        local,
        mesh=mesh,
        in_specs=(P(None, None, "gx", "gy"), P(None, None, "gx", "gy"), P()),
        out_specs=P(None, None, "gx", "gy"),
        check_vma=False,
    )
```

profile of v0, /device:TPU:0, one launch (start us, length us, event | category | flops | bytes accessed | tf_op | source)
XLA Modules:
  0.0 58.7 jit_solution(11839898208377386604)
XLA Ops:
  0.0 0.8 %fusion = (f32[1,8,32,128]{3,2,1,0:T(8,128)S(1)}, f32[8,32,128]{2,1,0:T(8,128)S(1)}) fusion(bf16[4,32,128]{2,1,0:T(8,128)(2,1)} %bitcast.10, bf16[4,32,128]{2,1,0:T(8,128)(2,1)} %bitcast.11), kind=kLoop, calls=%fused_computation.2 | loop fusion | flops 65536 | bytes 327680 | tf_op jit(solution)/shard_map/stack | solution.py:713
  0.8 3.0 %collective-permute-start = (f32[8,32,128]{2,1,0:T(8,128)S(1)}, f32[8,32,128]{2,1,0:T(8,128)S(1)}, u32[]{:S(2)}, u32[]{:S(2)}) collective-permute-start(f32[8,32,128]{2,1,0:T(8,128)S(1)} %get-tuple-element.46), channel_id=1, source_target_pairs={{0,2},{2,0},{4,6},{6,4},{8,10},{10,8},{12,14},{14,12},{16,18},{18,... | collective-permute-start | bytes 393224 | tf_op jit(solution)/shard_map/ppermute | solution.py:712
  3.8 0.7 %collective-permute-start.1 = (f32[8,32,128]{2,1,0:T(8,128)S(1)}, f32[8,32,128]{2,1,0:T(8,128)S(1)}, u32[]{:S(2)}, u32[]{:S(2)}) collective-permute-start(f32[8,32,128]{2,1,0:T(8,128)S(1)} %get-tuple-element.46), channel_id=1, source_target_pairs={{2,4},{4,2},{6,8},{8,6},{10,12},{12,10},{14,16},{16,14},{18,20},{2... | collective-permute-start | bytes 393224 | tf_op jit(solution)/shard_map/ppermute | solution.py:712
  4.5 2.8 %collective-permute-done = f32[8,32,128]{2,1,0:T(8,128)S(1)} collective-permute-done((f32[8,32,128]{2,1,0:T(8,128)S(1)}, f32[8,32,128]{2,1,0:T(8,128)S(1)}, u32[]{:S(2)}, u32[]{:S(2)}) %collective-permute-start) | collective-permute-done | bytes 131104 | tf_op jit(solution)/shard_map/ppermute | solution.py:712
  7.3 0.0 collective-permute-done.1
  7.4 2.5 %all-gather = f32[6,8,32,128]{3,2,1,0:T(8,128)} all-gather(f32[3,8,32,128]{3,2,1,0:T(8,128)S(1)} %pad_maximum_fusion), channel_id=2, replica_groups=mesh['gx'=16,'gy'=2] {'gy'}, dimensions={0}, use_global_device_ids=true | all-gather | bytes 1179648 | tf_op jit(solution)/shard_map/all_gather | solution.py:713
  9.9 7.2 %start_kernel.1 = (f32[2,2,2,104,128]{4,3,2,1,0:T(8,128)}, f32[2,2,1,56,128]{4,3,2,1,0:T(8,128)}, f32[1,2,1,32,128]{4,3,2,1,0:T(8,128)}, f32[2,2,2,104,128]{4,3,...) custom-call(f32[2,2]{1,0:T(2,128)} %refs_0_.1, ...), custom_call_target="tpu_custom_call" | custom-call | tf_op jit(solution)/shard_map/start_kernel/pallas_call | solution.py:750
  17.0 18.1 %all_to_all.10.refs_0_.refs_1_ = f32[16,1,16,128]{3,2,1,0:T(8,128)} all-to-all(f32[16,1,16,128]{3,2,1,0:T(8,128)} %get-tuple-element.25), channel_id=1, replica_groups=mesh['gx'=16,'gy'=2] {'gx'}, dimensions={0} | all-to-all | bytes 262144 | tf_op jit(solution)/shard_map/all_to_all | solution.py:753
  35.1 6.7 %middle_kernel.1 = (f32[2,2,2,104,128]{4,3,2,1,0:T(8,128)}, f32[2,2,1,56,128]{4,3,2,1,0:T(8,128)}, f32[1,2,1,32,128]{4,3,2,1,0:T(8,128)}, f32[2,2,1,56,128]{4,3,...) custom-call(f32[16,1,16,128]{3,2,1,0:T(8,128)} %all_to_all.10.refs_0, ...), custom_call_target="tpu_custom_call" | custom-call | tf_op jit(solution)/shard_map/middle_kernel/pallas_call | solution.py:755
  41.8 11.7 %all_to_all.11.refs_0_ = f32[16,1,8,128]{3,2,1,0:T(8,128)} all-to-all(f32[16,1,8,128]{3,2,1,0:T(8,128)} %get-tuple-element.37), channel_id=1, replica_groups=mesh['gx'=16,'gy'=2] {'gx'}, dimensions={0} | all-to-all | bytes 131072 | tf_op jit(solution)/shard_map/all_to_all | solution.py:758
  53.5 5.3 %last_kernel.1 = f32[2,2,32,128]{3,2,1,0:T(8,128)} custom-call(f32[16,1,8,128]{3,2,1,0:T(8,128)} %all_to_all.11.refs_0_, f32[16,1,16,128]{3,2,1,0:T(8,128)} %all_to_all.10.refs_0_.refs_1_, f32[2,2,2,104,128]{4,3,2,1,0:T(8,128)} %get-tuple-element.38.refs_2_, f32[2,2,1,56,128]{4,3,2,1,0:T(8,128)} %get-tuple-element.39.refs_3_, ...), custom_call_target="tpu_custom_call" | custom-call | tf_op jit(solution)/shard_map/last_kernel/pallas_call | solution.py:760
  (1 shorter events, 0.0 us)
Async XLA Ops:
  0.8 6.5 %collective-permute-start = (f32[8,32,128]{2,1,0:T(8,128)S(1)}, f32[8,32,128]{2,1,0:T(8,128)S(1)}, u32[]{:S(2)}, u32[]{:S(2)}) collective-permute-start(f32[8,32,128]{2,1,0:T(8,128)S(1)} %get-tuple-element.46), channel_id=1, source_target_pairs={{0,2},{2,0},{4,6},{6,4},{8,10},{10,8},{12,14},{14,12},{16,18},{18,... | collective-permute-start | bytes 393224 | tf_op jit(solution)/shard_map/ppermute | solution.py:712
  3.8 3.5 %collective-permute-start.1 = (f32[8,32,128]{2,1,0:T(8,128)S(1)}, f32[8,32,128]{2,1,0:T(8,128)S(1)}, u32[]{:S(2)}, u32[]{:S(2)}) collective-permute-start(f32[8,32,128]{2,1,0:T(8,128)S(1)} %get-tuple-element.46), channel_id=1, source_target_pairs={{2,4},{4,2},{6,8},{8,6},{10,12},{12,10},{14,16},{16,14},{18,20},{2... | collective-permute-start | bytes 393224 | tf_op jit(solution)/shard_map/ppermute | solution.py:712
where the time goes:
time: 59.1 us; the launch traced here: 58.7 us
  blocking collectives  32.3 us (55%)
  Pallas kernels  19.1 us (32%)
  starting transfers between devices  3.69 us (6%)
  waiting for transfers between devices  2.83 us (5%)
  other arithmetic  0.82 us (1%)
    all_to_all x1, blocking collectives, local(): first_received = lax.all_to_all(message, 'gx', 0, 0, tiled=True)  18.1 us
    all_to_all x1, blocking collectives, local(): received = lax.all_to_all(message, 'gx', 0, 0, tiled=True)  11.7 us
    pallas_call x1, Pallas kernels, local(): call(start_kernel, outs, rests, specs)(mixing, whole)  7.16 us
    pallas_call x1, Pallas kernels, local(): call(middle_kernel, outs, coarse + rests)  6.66 us
    pallas_call x1, Pallas kernels, local(): call(last_kernel, outs, [vmem(shape) for shape in fields] + coarse)  5.25 us
    ppermute x2, starting transfers between devices, local(): beside = [lax.ppermute(raw, 'gx', far), lax.ppermute(raw, 'gx', near)][::-1]  3.69 us
    ppermute x2, waiting for transfers between devices, local(): beside = [lax.ppermute(raw, 'gx', far), lax.ppermute(raw, 'gx', near)][::-1]  2.83 us
    all_gather x1, blocking collectives, local(): whole = lax.all_gather(jnp.stack([raw] + beside), 'gy')  2.5 us
  transfers between devices with their start and end apart: 2, of which 1 were waited for; matrix products, arithmetic and copies ran while one was open for 0% of the time, Pallas kernels for 0%

commit v1 on v0

--- a/solution.py
+++ b/solution.py
@@ -551,7 +551,7 @@
     row_index, ends = domain_ends(sizes)
     for grid, ref in zip(grids, (u0, u1, u2)):
         zero_margin(grid, ref)
-    m = [[mixing[i, j] for j in range(2)] for i in range(2)]
+    m = [[mixing[2 * i + j] for j in range(2)] for i in range(2)]
     water = [m[0][0] * m[0][0], m[1][0] * m[1][0]]
     cross = [m[0][0] * m[0][1], m[1][0] * m[1][1]]
     bone = [m[0][1] * m[0][1], m[1][1] * m[1][1]]
@@ -734,22 +734,23 @@
         vmem(fields[2]),
     ]
 
-    def call(body, outs, scratch, in_specs=None):
+    vmem_limit = min(16 * max(1, sizes.tiles), 60) << 20
+
+    def call(body, outs, scratch):
         kernel = lambda *refs: body(Sizes(*extents), *refs)
-        extra = {} if in_specs is None else {"in_specs": in_specs}
         return pl.pallas_call(
             kernel,
             out_shape=[shaped(shape) for shape in outs],
             scratch_shapes=scratch,
             name=body.__name__,
-            **extra,
+            compiler_params=pltpu.CompilerParams(vmem_limit_bytes=vmem_limit),
         )
 
     outs = fields + fields + datas + fields[1:] + [message_shape(4)]
-    specs = [pl.BlockSpec(memory_space=pltpu.SMEM), pl.BlockSpec(memory_space=pltpu.VMEM)]
+    spread = jnp.broadcast_to(mixing.reshape(-1, 1, 1), (mixing.size, SUB, LANES))
     u0, u1, u2, f0, f1, f2, d0, d1, d2, uc1, uc2, message = call(
-        start_kernel, outs, rests, specs
-    )(mixing, whole)
+        start_kernel, outs, rests
+    )(spread, whole)
     first_received = lax.all_to_all(message, "gx", 0, 0, tiled=True)
     outs = fields + fields[1:] + fields[1:] + [message_shape(2)]
     u0, u1, u2, f1, f2, uc1, uc2, message = call(middle_kernel, outs, coarse + rests)(

time: 59.1 us -> 51.4 us (0.87)
  Pallas kernels: 19.1 us -> 13.1 us
  blocking collectives: 32.3 us -> 30.6 us
    pallas_call x1, Pallas kernels: 6.66 us -> 4.37 us  [local(): call(middle_kernel, outs, coarse + rests)]
    pallas_call x1, Pallas kernels: 7.16 us -> 5.09 us  [local(): call(start_kernel, outs, rests)(spread, whole)]
    pallas_call x1, Pallas kernels: 5.25 us -> 3.64 us  [local(): call(last_kernel, outs, [vmem(shape) for shape in fields] + coarse)]
    all_to_all x1, blocking collectives: 11.7 us -> 10.4 us  [local(): received = lax.all_to_all(message, 'gx', 0, 0, tiled=True)]
where the time goes in v1:
time: 51.4 us; the launch traced here: 51.2 us
  blocking collectives  30.6 us (60%)
  Pallas kernels  13.1 us (25%)
  starting transfers between devices  3.69 us (7%)
  waiting for transfers between devices  2.74 us (5%)
  other arithmetic  0.82 us (2%)
    all_to_all x1, blocking collectives, local(): first_received = lax.all_to_all(message, 'gx', 0, 0, tiled=True)  17.8 us
    all_to_all x1, blocking collectives, local(): received = lax.all_to_all(message, 'gx', 0, 0, tiled=True)  10.4 us
    pallas_call x1, Pallas kernels, local(): call(start_kernel, outs, rests)(spread, whole)  5.09 us
    pallas_call x1, Pallas kernels, local(): call(middle_kernel, outs, coarse + rests)  4.37 us
    ppermute x2, starting transfers between devices, local(): beside = [lax.ppermute(raw, 'gx', far), lax.ppermute(raw, 'gx', near)][::-1]  3.69 us
    pallas_call x1, Pallas kernels, local(): call(last_kernel, outs, [vmem(shape) for shape in fields] + coarse)  3.64 us
    ppermute x2, waiting for transfers between devices, local(): beside = [lax.ppermute(raw, 'gx', far), lax.ppermute(raw, 'gx', near)][::-1]  2.74 us
    all_gather x1, blocking collectives, local(): whole = lax.all_gather(jnp.stack([raw] + beside), 'gy')  2.37 us
  transfers between devices with their start and end apart: 2, of which 1 were waited for; matrix products, arithmetic and copies ran while one was open for 0% of the time, Pallas kernels for 0%

profile of v1, /device:TPU:0, one launch (start us, length us, event | category | flops | bytes accessed | tf_op | source)
XLA Modules:
  0.0 51.2 jit_solution(10504016737301488446)
XLA Ops:
  0.0 0.8 %fusion = (f32[1,8,32,128]{3,2,1,0:T(8,128)S(1)}, f32[8,32,128]{2,1,0:T(8,128)S(1)}) fusion(bf16[4,32,128]{2,1,0:T(8,128)(2,1)} %bitcast.10, bf16[4,32,128]{2,1,0:T(8,128)(2,1)} %bitcast.11), kind=kLoop, calls=%fused_computation.2 | loop fusion | flops 65536 | bytes 327680 | tf_op jit(solution)/shard_map/stack | solution.py:713
  0.8 0.0 copy-start
  0.8 3.0 %collective-permute-start = (f32[8,32,128]{2,1,0:T(8,128)S(1)}, f32[8,32,128]{2,1,0:T(8,128)S(1)}, u32[]{:S(2)}, u32[]{:S(2)}) collective-permute-start(f32[8,32,128]{2,1,0:T(8,128)S(1)} %get-tuple-element.46), channel_id=1, source_target_pairs={{0,2},{2,0},{4,6},{6,4},{8,10},{10,8},{12,14},{14,12},{16,18},{18,... | collective-permute-start | bytes 393224 | tf_op jit(solution)/shard_map/ppermute | solution.py:712
  3.8 0.7 %collective-permute-start.1 = (f32[8,32,128]{2,1,0:T(8,128)S(1)}, f32[8,32,128]{2,1,0:T(8,128)S(1)}, u32[]{:S(2)}, u32[]{:S(2)}) collective-permute-start(f32[8,32,128]{2,1,0:T(8,128)S(1)} %get-tuple-element.46), channel_id=1, source_target_pairs={{2,4},{4,2},{6,8},{8,6},{10,12},{12,10},{14,16},{16,14},{18,20},{2... | collective-permute-start | bytes 393224 | tf_op jit(solution)/shard_map/ppermute | solution.py:712
  4.5 0.0 copy-done
  4.5 0.1 broadcast_in_dim.7
  4.6 2.7 %collective-permute-done = f32[8,32,128]{2,1,0:T(8,128)S(1)} collective-permute-done((f32[8,32,128]{2,1,0:T(8,128)S(1)}, f32[8,32,128]{2,1,0:T(8,128)S(1)}, u32[]{:S(2)}, u32[]{:S(2)}) %collective-permute-start) | collective-permute-done | bytes 131104 | tf_op jit(solution)/shard_map/ppermute | solution.py:712
  7.3 0.0 collective-permute-done.1
  7.4 2.4 %all-gather = f32[6,8,32,128]{3,2,1,0:T(8,128)S(1)} all-gather(f32[3,8,32,128]{3,2,1,0:T(8,128)S(1)} %pad_maximum_fusion), channel_id=2, replica_groups=mesh['gx'=16,'gy'=2] {'gy'}, dimensions={0}, use_global_device_ids=true | all-gather | bytes 1179648 | tf_op jit(solution)/shard_map/all_gather | solution.py:713
  9.7 0.1 broadcast_in_dim.8.refs_0_
  9.8 5.1 %start_kernel.1 = (f32[2,2,2,104,128]{4,3,2,1,0:T(8,128)S(1)}, f32[2,2,1,56,128]{4,3,2,1,0:T(8,128)S(1)}, f32[1,2,1,32,128]{4,3,2,1,0:T(8,128)S(1)}, f32[2,2,2,1...) custom-call(f32[4,8,128]{2,1,0:T(8,128)S(1)} %broadcast_in_dim.8.ref, ...), custom_call_target="tpu_custom_call" | custom-call | tf_op jit(solution)/shard_map/start_kernel/pallas_call | solution.py:751
  14.9 17.8 %all_to_all.10.refs_0_.refs_1_ = f32[16,1,16,128]{3,2,1,0:T(8,128)S(1)} all-to-all(f32[16,1,16,128]{3,2,1,0:T(8,128)S(1)} %get-tuple-element.25), channel_id=1, replica_groups=mesh['gx'=16,'gy'=2] {'gx'}, dimensions={0} | all-to-all | bytes 262144 | tf_op jit(solution)/shard_map/all_to_all | solution.py:754
  32.7 4.4 %middle_kernel.1 = (f32[2,2,2,104,128]{4,3,2,1,0:T(8,128)S(1)}, f32[2,2,1,56,128]{4,3,2,1,0:T(8,128)S(1)}, f32[1,2,1,32,128]{4,3,2,1,0:T(8,128)S(1)}, f32[2,2,1,...) custom-call(f32[16,1,16,128]{3,2,1,0:T(8,128)S(1)} %all_to_all.10.re, ...), custom_call_target="tpu_custom_call" | custom-call | tf_op jit(solution)/shard_map/middle_kernel/pallas_call | solution.py:756
  37.1 10.4 %all_to_all.11.refs_0_ = f32[16,1,8,128]{3,2,1,0:T(8,128)S(1)} all-to-all(f32[16,1,8,128]{3,2,1,0:T(8,128)S(1)} %get-tuple-element.37), channel_id=1, replica_groups=mesh['gx'=16,'gy'=2] {'gx'}, dimensions={0} | all-to-all | bytes 131072 | tf_op jit(solution)/shard_map/all_to_all | solution.py:759
  47.5 3.6 %last_kernel.1 = f32[2,2,32,128]{3,2,1,0:T(8,128)} custom-call(f32[16,1,8,128]{3,2,1,0:T(8,128)S(1)} %all_to_all.11.refs_0_, f32[16,1,16,128]{3,2,1,0:T(8,128)S(1)} %all_to_all.10.refs_0_.refs_1_, f32[2,2,2,104,128]{4,3,2,1,0:T(8,128)S(1)} %get-tuple-element.38.refs_2_, f32[2,2,1,56,128]{4,3,2,1,0:T(8,128)S(1)} %get-tuple-element.39.refs_3_, ...), custom_call_target="tpu_custom_call" | custom-call | tf_op jit(solution)/shard_map/last_kernel/pallas_call | solution.py:761
  (1 shorter events, 0.0 us)
Async XLA Ops:
  0.8 3.7 %copy-start = (f32[2,2]{1,0:T(2,128)S(1)}, f32[2,2]{1,0:T(2,128)}, u32[]{:S(2)}) copy-start(f32[2,2]{1,0:T(2,128)} %param.5) | copy-start | bytes 52
  0.8 6.5 %collective-permute-start = (f32[8,32,128]{2,1,0:T(8,128)S(1)}, f32[8,32,128]{2,1,0:T(8,128)S(1)}, u32[]{:S(2)}, u32[]{:S(2)}) collective-permute-start(f32[8,32,128]{2,1,0:T(8,128)S(1)} %get-tuple-element.46), channel_id=1, source_target_pairs={{0,2},{2,0},{4,6},{6,4},{8,10},{10,8},{12,14},{14,12},{16,18},{18,... | collective-permute-start | bytes 393224 | tf_op jit(solution)/shard_map/ppermute | solution.py:712
  3.8 3.5 %collective-permute-start.1 = (f32[8,32,128]{2,1,0:T(8,128)S(1)}, f32[8,32,128]{2,1,0:T(8,128)S(1)}, u32[]{:S(2)}, u32[]{:S(2)}) collective-permute-start(f32[8,32,128]{2,1,0:T(8,128)S(1)} %get-tuple-element.46), channel_id=1, source_target_pairs={{2,4},{4,2},{6,8},{8,6},{10,12},{12,10},{14,16},{16,14},{18,20},{2... | collective-permute-start | bytes 393224 | tf_op jit(solution)/shard_map/ppermute | solution.py:712

commit v2 on v1

--- a/solution.py
+++ b/solution.py
@@ -62,8 +62,12 @@
 def flux(gap, with_factor):
     if not with_factor:
         return jnp.clip(gap, -huber_delta, huber_delta), None
-    factor = huber_delta / jnp.maximum(jnp.abs(gap), huber_delta)
+    factor = 1.0 / jnp.maximum(jnp.abs(gap), huber_delta)
     return factor * gap, factor
+
+
+def scaled_penalty(level, with_factor):
+    return penalty_of(level) * huber_delta if with_factor else penalty_of(level)
 
 
 def keep(mask, value):
@@ -219,7 +223,7 @@
 
 
 def relax_strips(grid, ends, field, source, data, first, last):
-    p = grid.penalty
+    p = scaled_penalty(grid.level, True)
 
     def emit(group, start, centers, flows, factors):
         rows = pl.ds(start, SUB)
@@ -240,7 +244,7 @@
 
 
 def first_relax_strips(grid, ends, field, source, data, first, last):
-    p = grid.penalty
+    p = scaled_penalty(grid.level, True)
 
     def emit(group, start, centers, flows, factors):
         rows = pl.ds(start, SUB)
@@ -264,7 +268,7 @@
 
 
 def residual_strips(grid, ends, field, source, data, out, first, last):
-    p = grid.penalty
+    p = scaled_penalty(grid.level, False)
 
     def emit(group, start, centers, flows, factors):
         rows = pl.ds(start, SUB)
@@ -370,113 +374,171 @@
 
 
 def coarse_correction(sizes, fields):
-    tiles = sizes.join_tiles
-    rows = sizes.row_devices * sizes.join_rows
+    tiles = max(1, sizes.join_tiles // 2)
     width = sizes.join_width
-    shape = (rows, LANES)
-    row, lane = row_of(shape), lane_of(shape)
-
-    def partner(values):
-        if len(values) == 1:
-            return [roll_lanes(values[0], LANES // 2)]
-        half = len(values) // 2
-        return values[half:] + values[:half]
+    lane, row = lane_of(), row_of()
+    low = lane < LANES // 2
+
+    def each(function, *values):
+        return [
+            [function(*(value[k][v] for value in values)) for v in range(len(values[0][0]))]
+            for k in range(tiles)
+        ]
+
+    def split(values):
+        if sizes.join_tiles > 1:
+            return values[:tiles], values[tiles:]
+        other = each(lambda x: roll_lanes(x, LANES // 2), values)
+        return (
+            each(lambda x, y: jnp.where(low, x, y), values, other),
+            each(lambda x, y: jnp.where(low, y, x), values, other),
+        )
+
+    def join(first, second):
+        if sizes.join_tiles > 1:
+            return first + second
+        return each(lambda x, y: jnp.where(low, x, y), first, second)
 
     def mean(values, step):
         pair = (lane & step) == 0
-        right, left = from_right(values, step), from_left(values, step)
-        values = [x + jnp.where(pair, r, s) for x, r, s in zip(values, right, left)]
-        pair = (row & step) == 0
-        return [
-            0.25 * (x + jnp.where(pair, roll_rows(x, -step), roll_rows(x, step))) for x in values
-        ]
+        result = [[] for _ in range(tiles)]
+        for v in range(0, len(values[0]), 2):
+            added = [value[v] + value[v + 1] for value in values]
+            right, left = from_right(added, step), from_left(added, step)
+            for k in range(tiles):
+                result[k].append(0.25 * (added[k] + jnp.where(pair, right[k], left[k])))
+        return result
+
+    def add(first, second):
+        return each(lambda a, b: a + b, first, second)
+
+    def subtract(first, second):
+        return each(lambda a, b: a - b, first, second)
 
     estimate, rest, diagonal, cross = fields
-    diagonals, crosses = [diagonal], [cross]
+    matrices = [(*split(diagonal), cross[:tiles])]
     for level in range(JOIN + 1, LEVELS):
         step = 1 << (level - JOIN - 1)
-        diagonals.append(mean(diagonals[-1], step))
-        crosses.append(mean(crosses[-1], step))
+        matrices.append(tuple(mean(part, step) for part in matrices[-1]))
 
     def sums(level, values, with_factor):
         step = 1 << (level - JOIN)
-        masks = [(lane + k * LANES) % width < width - step for k in range(tiles)]
-        flow_sum, factor_sum = row_sums(values, masks, with_factor, step)
-        below = row < rows - step
+        count = len(values[0])
+        totals = [[[None] * count for _ in range(tiles)] for _ in range(2)]
+        for v in range(count):
+            line = [value[v] for value in values]
+            for shifted, side in ((from_right(line, step), 1), (from_left(line, step), 0)):
+                for k in range(tiles):
+                    place = (lane + k * LANES) % width
+                    inside = place < width - step if side else place >= step
+                    for total, part in zip(totals, flux(shifted[k] - line[k], with_factor)):
+                        part = keep(inside, part)
+                        total[k][v] = part if side or part is None else total[k][v] + part
         for k, value in enumerate(values):
-            flow, factor = flux(roll_rows(value, -step) - value, with_factor)
-            flow = keep(below, flow)
-            flow_sum[k] = flow_sum[k] + (flow - roll_rows(flow, step))
-            if with_factor:
-                factor = keep(below, factor)
-                factor_sum[k] = factor_sum[k] + (factor + roll_rows(factor, step))
-        return flow_sum, factor_sum
-
-    def apply(level, values, flow_sum):
-        p = penalty_of(level)
-        other = partner(values)
-        d, x = diagonals[level - JOIN], crosses[level - JOIN]
-        return [
-            d[k] * values[k] + x[k] * other[k] - p * flow_sum[k] for k in range(tiles)
-        ]
-
-    def solve(level, values, factor_sum, right):
-        p = penalty_of(level)
-        d, x = diagonals[level - JOIN], crosses[level - JOIN]
-        h = [d[k] + p * factor_sum[k] for k in range(tiles)]
-        h_other, r_other = partner(h), partner(right)
-        return [
-            values[k]
-            + relaxation
-            / (h[k] * h_other[k] - x[k] * x[k])
-            * (h_other[k] * right[k] - x[k] * r_other[k])
-            for k in range(tiles)
-        ]
+            edges = [
+                flux(b - a, with_factor) for a, b in zip(value, value[1:])
+            ]
+            first = flux(roll_rows(value[-1], 1) - value[0], with_factor)
+            last = flux(roll_rows(value[0], -1) - value[-1], with_factor)
+            for place in range(2 if with_factor else 1):
+                total = totals[place][k]
+                for v, edge in enumerate(edges):
+                    total[v] = total[v] + edge[place]
+                    opposite = edge[place] if place else -edge[place]
+                    total[v + 1] = total[v + 1] + opposite
+                total[0] = total[0] + keep(row > 0, first[place])
+                total[-1] = total[-1] + keep(row < SUB - 1, last[place])
+        return totals
+
+    def apply(level, values, flows, with_factor):
+        p = scaled_penalty(level, with_factor)
+        water, bone, cross = matrices[level - JOIN]
+        take = lambda d, x, own, other, flow: d * own + x * other - p * flow
+        return (
+            each(take, water, cross, values[0], values[1], flows[0]),
+            each(take, bone, cross, values[1], values[0], flows[1]),
+        )
+
+    def solve(level, values, factors, right):
+        p = scaled_penalty(level, True)
+        water, bone, cross = matrices[level - JOIN]
+        water = each(lambda d, factor: d + p * factor, water, factors[0])
+        bone = each(lambda d, factor: d + p * factor, bone, factors[1])
+        scale = each(lambda a, b, x: relaxation / (a * b - x * x), water, bone, cross)
+        move = lambda own, s, b, x, r, q: own + s * (b * r - x * q)
+        return (
+            each(move, values[0], scale, bone, cross, right[0], right[1]),
+            each(move, values[1], scale, water, cross, right[1], right[0]),
+        )
+
+    def both(function, *pairs):
+        return tuple(function(*(pair[m] for pair in pairs)) for m in range(2))
+
+    def image_of(level, values, with_factor):
+        totals = [sums(level, value, with_factor) for value in values]
+        image = apply(level, values, [total[0] for total in totals], with_factor)
+        return image, [total[1] for total in totals]
 
     def relax(level, values, source):
-        flow_sum, factor_sum = sums(level, values, True)
-        image = apply(level, values, flow_sum)
-        return solve(level, values, factor_sum, [a - b for a, b in zip(source, image)])
+        image, factors = image_of(level, values, True)
+        return solve(level, values, factors, both(subtract, source, image))
 
     def cycle(level, values, rest):
-        flow_sum, factor_sum = sums(level, values, True)
-        image = apply(level, values, flow_sum)
-        source = [a + b for a, b in zip(rest, image)]
+        image, factors = image_of(level, values, True)
+        source = both(add, rest, image)
         start = values
-        values = solve(level, values, factor_sum, rest)
+        values = solve(level, values, factors, rest)
         if level == LEVELS - 1:
             for _ in range(COARSE_SWEEPS - 1):
                 values = relax(level, values, source)
         else:
             step = 1 << (level - JOIN)
-            image = apply(level, values, sums(level, values, False)[0])
-            coarse_rest = mean([a - b for a, b in zip(source, image)], step)
-            correction = cycle(level + 1, mean(values, step), coarse_rest)
-            values = relax(level, [a + b for a, b in zip(values, correction)], source)
-        return [a - b for a, b in zip(values, start)]
-
-    return cycle(JOIN, estimate, rest)
+            image, _ = image_of(level, values, False)
+            coarse_rest = [mean(part, step) for part in both(subtract, source, image)]
+            coarse = [mean(part, step) for part in values]
+            correction = cycle(level + 1, coarse, coarse_rest)
+            raised = [
+                [[part[v // 2] for v in range(2 * len(part))] for part in member]
+                for member in correction
+            ]
+            values = relax(level, both(add, values, raised), source)
+        return both(subtract, values, start)
+
+    return join(*cycle(JOIN, split(estimate), split(rest)))
 
 
 def ascend(sizes, ends, row_index, received, state, scratch, level_rows):
     grids = sizes.grids
     u, f, d, uc = state
-    gathered, correction, raised = scratch
+    correction, raised = scratch
     h = sizes.join_rows
     whole = sizes.row_devices * h
+    count = whole // SUB
     fields = []
-    for place, (ref, field) in enumerate(received):
-        tiles = []
-        for k in range(sizes.join_tiles):
-            for source in range(sizes.row_devices):
-                gathered[place, k, pl.ds(source * h, h), :] = ref[source, k, pl.ds(field * h, h), :]
-            tiles.append(gathered[place, k])
-        fields.append(tiles)
+    for ref, field, total in received:
+        block = sizes.join_tiles * total * h
+        fields.append(
+            [
+                [
+                    ref[
+                        pl.ds(
+                            v // h * block + (k * total + field) * h + v % h,
+                            SUB,
+                            stride=count // h * block,
+                        ),
+                        :,
+                    ]
+                    for v in range(count)
+                ]
+                for k in range(sizes.join_tiles)
+            ]
+        )
     values = coarse_correction(sizes, fields)
     for k in range(sizes.join_tiles):
         correction[k, :SUB, :] = jnp.zeros((SUB, LANES), jnp.float32)
-        correction[k, pl.ds(SUB, whole), :] = values[k]
         correction[k, pl.ds(SUB + whole, 2 * SUB), :] = jnp.zeros((2 * SUB, LANES), jnp.float32)
+        for v in range(count):
+            correction[k, pl.ds(SUB + v, SUB, stride=count), :] = values[k][v]
 
     grid = grids[2]
     strips = grid.rows // SUB
@@ -546,7 +608,30 @@
     return row_index, (row_index > 0, row_index < sizes.row_devices - 1)
 
 
-def start_kernel(sizes, mixing, raw, u0, u1, u2, f0, f1, f2, d0, d1, d2, uc1, uc2, message, *rest):
+def split_columns(sizes, pieces, swapped, out):
+    shape = (2 * LANES, 2 * LANES)
+    source, target = row_of(shape), lane_of(shape)
+    source = jnp.bitwise_xor(source, swapped * LANES)
+    wanted = jnp.where(target < LANES, 2 * target, 2 * (target - LANES) + 1)
+    select = (source == wanted).astype(jnp.float32).astype(jnp.bfloat16)
+    for tile in range(sizes.tiles):
+        for part in range(3):
+            sides = [piece[part] for piece in pieces[2 * tile : 2 * tile + 2]]
+            sides = [side.reshape(-1, LANES).astype(jnp.bfloat16) for side in sides]
+            both = jnp.concatenate(sides, axis=1)
+            result = jnp.dot(both, select, preferred_element_type=jnp.float32)
+            out[tile, part] = result.reshape(out.shape[2:])
+
+
+def start_kernel(sizes, mixing, *refs):
+    if sizes.column_devices == 2:
+        pieces, refs = refs[:2], refs[2:]
+        swapped = lax.axis_index("gy")
+    else:
+        pieces, refs = [refs[0].at[k] for k in range(sizes.column_devices)], refs[1:]
+        swapped = 0
+    u0, u1, u2, f0, f1, f2, d0, d1, d2, uc1, uc2, message, ordered, *rest = refs
+    split_columns(sizes, pieces, swapped, ordered)
     grids = sizes.grids
     row_index, ends = domain_ends(sizes)
     for grid, ref in zip(grids, (u0, u1, u2)):
@@ -564,9 +649,6 @@
     )
     grid = grids[0]
     lane, row = lane_of(), row_of()
-    low = lane < LANES // 2
-    even_first = jnp.where(low, 2 * lane, 2 * lane - LANES + 1)
-    odd_first = jnp.where(low, 2 * lane + 1, 2 * lane - LANES)
     half = sizes.tiles
     p = grid.penalty
     for group in range(grid.groups):
@@ -576,18 +658,14 @@
 
             def load(kind, energy, tile):
                 plane = (2 * kind + energy) * sizes.slices + group
-                pieces = [
-                    raw[2 * tile + side, parts[part], plane, pl.ds(inner, SUB), :]
+                rows = pl.ds(inner, SUB)
+                sides = [
+                    ordered[tile, parts[part], plane, rows, pl.ds(side * LANES, LANES)]
                     for side in range(2)
                 ]
                 if kind == 1 and beyond[part] is not None:
-                    pieces = [piece + beyond[part] for piece in pieces]
-                first = take_lanes(pieces[0], even_first)
-                second = take_lanes(pieces[1], odd_first)
-                return (
-                    jnp.where(low, first, second),
-                    roll_lanes(jnp.where(low, second, first), LANES // 2),
-                )
+                    sides = [side + beyond[part] for side in sides]
+                return sides
 
             vertical = jnp.full((SUB, LANES), 2.0, jnp.float32)
             for edge, inside in zip((grid.own - 1, 2 * grid.own - 1), ends):
@@ -639,14 +717,14 @@
 def middle_kernel(
     sizes, received, u0i, u1i, u2i, f0, f1i, f2i, d0, d1, d2, uc1i, uc2i,
     u0, u1, u2, f1, f2, uc1, uc2, message,
-    gathered, correction, raised0, raised1, raised2, *rest,
+    correction, raised0, raised1, raised2, *rest,
 ):
     grids = sizes.grids
     row_index, ends = domain_ends(sizes)
     for source, target in ((u0i, u0), (u1i, u1), (u2i, u2)):
         target[...] = source[...]
-    scratch = (gathered, correction, (raised0, raised1, raised2))
-    fields = [(received, k) for k in range(4)]
+    scratch = (correction, (raised0, raised1, raised2))
+    fields = [(received, k, 4) for k in range(4)]
     span = middle_rows(sizes)
     state = ((u0, u1, u2), (f0, f1i, f2i), (d0, d1, d2), (None, uc1i, uc2i))
     ascend(sizes, ends, row_index, fields, state, scratch, span)
@@ -661,14 +739,14 @@
 def last_kernel(
     sizes, received, first_received, u0, u1, u2, f0, f1, f2, d0, d1, d2, uc1, uc2,
     out,
-    v0, v1, v2, gathered, correction, raised0, raised1, raised2,
+    v0, v1, v2, correction, raised0, raised1, raised2,
 ):
     grids = sizes.grids
     row_index, ends = domain_ends(sizes)
     for source, target in ((u0, v0), (u1, v1), (u2, v2)):
         target[...] = source[...]
-    scratch = (gathered, correction, (raised0, raised1, raised2))
-    fields = [(received, 0), (received, 1), (first_received, 2), (first_received, 3)]
+    scratch = (correction, (raised0, raised1, raised2))
+    fields = [(received, k, 2) for k in range(2)] + [(first_received, k, 4) for k in (2, 3)]
     own = (sizes.rows // SUB, 2 * sizes.rows // SUB)
     span = (own, middle_rows(sizes)[1])
     state = ((v0, v1, v2), (f0, f1, f2), (d0, d1, d2), (None, uc1, uc2))
@@ -710,7 +788,11 @@
     for i in range(row_devices - 1):
         (far if i % 2 else near).extend([(i, i + 1), (i + 1, i)])
     beside = [lax.ppermute(raw, "gx", far), lax.ppermute(raw, "gx", near)][::-1]
-    whole = lax.all_gather(jnp.stack([raw] + beside), "gy")
+    tiles = jnp.stack([raw] + beside)
+    if column_devices == 2:
+        pieces = (tiles, lax.ppermute(tiles, "gy", [(0, 1), (1, 0)]))
+    else:
+        pieces = (lax.all_gather(tiles, "gy"),)
 
     def vmem(shape):
         return pltpu.VMEM(shape, jnp.float32)
@@ -727,7 +809,6 @@
     rests = [vmem(halved(fields[0])), vmem(fields[1]), vmem(fields[2])]
     join_whole = row_devices * sizes.join_rows
     coarse = [
-        vmem((4, sizes.join_tiles, join_whole, LANES)),
         vmem((sizes.join_tiles, join_whole + 3 * SUB, LANES)),
         vmem(halved(fields[0])),
         vmem(fields[1]),
@@ -749,14 +830,14 @@
     outs = fields + fields + datas + fields[1:] + [message_shape(4)]
     spread = jnp.broadcast_to(mixing.reshape(-1, 1, 1), (mixing.size, SUB, LANES))
     u0, u1, u2, f0, f1, f2, d0, d1, d2, uc1, uc2, message = call(
-        start_kernel, outs, rests
-    )(spread, whole)
-    first_received = lax.all_to_all(message, "gx", 0, 0, tiled=True)
+        start_kernel, outs, [vmem((sizes.tiles,) + tiles.shape[:3] + (2 * LANES,))] + rests
+    )(spread, *pieces)
+    first_received = lax.all_to_all(message, "gx", 0, 0, tiled=True).reshape(-1, LANES)
     outs = fields + fields[1:] + fields[1:] + [message_shape(2)]
     u0, u1, u2, f1, f2, uc1, uc2, message = call(middle_kernel, outs, coarse + rests)(
         first_received, u0, u1, u2, f0, f1, f2, d0, d1, d2, uc1, uc2
     )
-    received = lax.all_to_all(message, "gx", 0, 0, tiled=True)
+    received = lax.all_to_all(message, "gx", 0, 0, tiled=True).reshape(-1, LANES)
     outs = [(2, slices, rows, columns)]
     return call(last_kernel, outs, [vmem(shape) for shape in fields] + coarse)(
         received, first_received, u0, u1, u2, f0, f1, f2, d0, d1, d2, uc1, uc2

time: 51.4 us -> 45.4 us (0.88)
  Pallas kernels: 13.1 us -> 7.65 us
  blocking collectives: 30.6 us -> 28.2 us
  waiting for transfers between devices: 2.74 us -> 3.89 us
  local copies, waits for them, and re-layouts: 0.16 us -> 0.72 us
    pallas_call x1, Pallas kernels: 5.09 us -> 1.55 us  [local(): call(start_kernel, outs, [vmem((sizes.tiles,) + tiles.shape[:3] + (2 * LA...]
    all_gather x1 -> x0, blocking collectives: 2.37 us -> none  [local(): whole = lax.all_gather(jnp.stack([raw] + beside), 'gy')]
    ppermute x0 -> x1, waiting for transfers between devices: none -> 1.06 us  [local(): pieces = (tiles, lax.ppermute(tiles, 'gy', [(0, 1), (1, 0)]))]
    pallas_call x1, Pallas kernels: 4.37 us -> 3.4 us  [local(): call(middle_kernel, outs, coarse + rests)]
    pallas_call x1, Pallas kernels: 3.64 us -> 2.71 us  [local(): call(last_kernel, outs, [vmem(shape) for shape in fields] + coarse)]
    unnamed x2, local copies, waits for them, and re-layouts: 0.01 us -> 0.57 us
  transfers between devices with their start and end apart: 2 -> 3, of which waited for: 1 -> 2; matrix products, arithmetic and copies ran while one was open for 0% -> 0% of each run, Pallas kernels for 0% -> 0%
where the time goes in v2:
time: 45.4 us; the launch traced here: 45.1 us
  blocking collectives  28.2 us (62%)
  Pallas kernels  7.65 us (17%)
  waiting for transfers between devices  3.89 us (9%)
  starting transfers between devices  3.76 us (8%)
  other arithmetic  0.82 us (2%)
  local copies, waits for them, and re-layouts  0.72 us (2%)
    all_to_all x2, blocking collectives, local(): lax.all_to_all(message, 'gx', 0, 0, tiled=True).reshape(-1, LANES)  28.2 us
    ppermute x2, starting transfers between devices, local(): beside = [lax.ppermute(raw, 'gx', far), lax.ppermute(raw, 'gx', near)][::-1]  3.69 us
    pallas_call x1, Pallas kernels, local(): call(middle_kernel, outs, coarse + rests)  3.4 us
    ppermute x2, waiting for transfers between devices, local(): beside = [lax.ppermute(raw, 'gx', far), lax.ppermute(raw, 'gx', near)][::-1]  2.83 us
    pallas_call x1, Pallas kernels, local(): call(last_kernel, outs, [vmem(shape) for shape in fields] + coarse)  2.71 us
    pallas_call x1, Pallas kernels, local(): call(start_kernel, outs, [vmem((sizes.tiles,) + tiles.shape[:3] + (2 * LA...  1.55 us
    ppermute x1, waiting for transfers between devices, local(): pieces = (tiles, lax.ppermute(tiles, 'gy', [(0, 1), (1, 0)]))  1.06 us
  transfers between devices with their start and end apart: 3, of which 2 were waited for; matrix products, arithmetic and copies ran while one was open for 0% of the time, Pallas kernels for 0%

profile of v2, /device:TPU:0, one launch (start us, length us, event | category | flops | bytes accessed | tf_op | source)
XLA Modules:
  0.0 45.1 jit_solution(11176232523333402378)
XLA Ops:
  0.0 0.8 %fusion = (f32[1,8,32,128]{3,2,1,0:T(8,128)S(1)}, f32[8,32,128]{2,1,0:T(8,128)S(1)}) fusion(bf16[4,32,128]{2,1,0:T(8,128)(2,1)} %bitcast.13, bf16[4,32,128]{2,1,0:T(8,128)(2,1)} %bitcast.14), kind=kLoop, calls=%fused_computation.2 | loop fusion | flops 65536 | bytes 327680 | tf_op jit(solution)/shard_map/stack | solution.py:791
  0.8 3.0 %collective-permute-start = (f32[8,32,128]{2,1,0:T(8,128)S(1)}, f32[8,32,128]{2,1,0:T(8,128)S(1)}, u32[]{:S(2)}, u32[]{:S(2)}) collective-permute-start(f32[8,32,128]{2,1,0:T(8,128)S(1)} %get-tuple-element.46), channel_id=1, source_target_pairs={{0,2},{2,0},{4,6},{6,4},{8,10},{10,8},{12,14},{14,12},{16,18},{18,... | collective-permute-start | bytes 393224 | tf_op jit(solution)/shard_map/ppermute | solution.py:790
  3.8 0.7 %collective-permute-start.1 = (f32[8,32,128]{2,1,0:T(8,128)S(1)}, f32[8,32,128]{2,1,0:T(8,128)S(1)}, u32[]{:S(2)}, u32[]{:S(2)}) collective-permute-start(f32[8,32,128]{2,1,0:T(8,128)S(1)} %get-tuple-element.46), channel_id=1, source_target_pairs={{2,4},{4,2},{6,8},{8,6},{10,12},{12,10},{14,16},{16,14},{18,20},{2... | collective-permute-start | bytes 393224 | tf_op jit(solution)/shard_map/ppermute | solution.py:790
  4.5 2.8 %collective-permute-done = f32[8,32,128]{2,1,0:T(8,128)S(1)} collective-permute-done((f32[8,32,128]{2,1,0:T(8,128)S(1)}, f32[8,32,128]{2,1,0:T(8,128)S(1)}, u32[]{:S(2)}, u32[]{:S(2)}) %collective-permute-start) | collective-permute-done | bytes 131104 | tf_op jit(solution)/shard_map/ppermute | solution.py:790
  7.3 0.0 collective-permute-done.1
  7.3 0.0 copy-start
  7.4 0.1 collective-permute-start.2
  7.4 0.6 %copy-done = f32[2,2]{1,0:T(2,128)S(1)} copy-done((f32[2,2]{1,0:T(2,128)S(1)}, f32[2,2]{1,0:T(2,128)}, u32[]{:S(2)}) %copy-start) | copy-done | bytes 40
  8.0 0.1 broadcast_in_dim.7
  8.1 1.1 %collective-permute-done.2.refs_2_ = f32[3,8,32,128]{3,2,1,0:T(8,128)S(1)} collective-permute-done((f32[3,8,32,128]{3,2,1,0:T(8,128)S(1)}, f32[3,8,32,128]{3,2,1,0:T(8,128)S(1)}, u32[]{:S(2)}, u32[]{:S(2)}) %collective-permute-start.2) | collective-permute-done | bytes 393248 | tf_op jit(solution)/shard_map/ppermute | solution.py:793
  9.2 0.1 broadcast_in_dim.8.refs_0_
  9.2 1.5 %start_kernel.1 = (f32[2,2,2,104,128]{4,3,2,1,0:T(8,128)S(1)}, f32[2,2,1,56,128]{4,3,2,1,0:T(8,128)S(1)}, f32[1,2,1,32,128]{4,3,2,1,0:T(8,128)S(1)}, f32[2,2,2,1...) custom-call(f32[4,8,128]{2,1,0:T(8,128)S(1)} %broadcast_in_dim.8.ref, ...), custom_call_target="tpu_custom_call" | custom-call | tf_op jit(solution)/shard_map/start_kernel/pallas_call | solution.py:832
  10.8 17.8 %all_to_all.10 = f32[16,1,16,128]{3,2,1,0:T(8,128)S(1)} all-to-all(f32[16,1,16,128]{3,2,1,0:T(8,128)S(1)} %get-tuple-element.25), channel_id=1, replica_groups=mesh['gx'=16,'gy'=2] {'gx'}, dimensions={0} | all-to-all | bytes 262144 | tf_op jit(solution)/shard_map/all_to_all | solution.py:835
  28.6 3.4 %middle_kernel.1 = (f32[2,2,2,104,128]{4,3,2,1,0:T(8,128)S(1)}, f32[2,2,1,56,128]{4,3,2,1,0:T(8,128)S(1)}, f32[1,2,1,32,128]{4,3,2,1,0:T(8,128)S(1)}, f32[2,2,1,...) custom-call(f32[256,128]{1,0:T(8,128)S(1)} %bitcast.8, ...), custom_call_target="tpu_custom_call" | custom-call | tf_op jit(solution)/shard_map/middle_kernel/pallas_call | solution.py:837
  32.0 10.4 %all_to_all.11 = f32[16,1,8,128]{3,2,1,0:T(8,128)S(1)} all-to-all(f32[16,1,8,128]{3,2,1,0:T(8,128)S(1)} %get-tuple-element.37), channel_id=1, replica_groups=mesh['gx'=16,'gy'=2] {'gx'}, dimensions={0} | all-to-all | bytes 131072 | tf_op jit(solution)/shard_map/all_to_all | solution.py:840
  42.4 2.7 %last_kernel.1 = f32[2,2,32,128]{3,2,1,0:T(8,128)} custom-call(f32[128,128]{1,0:T(8,128)S(1)} %bitcast.10, f32[256,128]{1,0:T(8,128)S(1)} %bitcast.9, f32[2,2,2,104,128]{4,3,2,1,0:T(8,128)S(1)} %get-tuple-element.38.refs_2_, f32[2,2,1,56,128]{4,3,2,1,0:T(8,128)S(1)} %get-tuple-element.39.refs_3_, f32[1,2,1,32,128]{4,3,2,1,0:T(8,128)S(1)} %get-tuple-element.40.refs_4_, ...), custom_call_target="tpu_custom_call" | custom-call | tf_op jit(solution)/shard_map/last_kernel/pallas_call | solution.py:842
  (1 shorter events, 0.0 us)
Async XLA Ops:
  0.8 6.5 %collective-permute-start = (f32[8,32,128]{2,1,0:T(8,128)S(1)}, f32[8,32,128]{2,1,0:T(8,128)S(1)}, u32[]{:S(2)}, u32[]{:S(2)}) collective-permute-start(f32[8,32,128]{2,1,0:T(8,128)S(1)} %get-tuple-element.46), channel_id=1, source_target_pairs={{0,2},{2,0},{4,6},{6,4},{8,10},{10,8},{12,14},{14,12},{16,18},{18,... | collective-permute-start | bytes 393224 | tf_op jit(solution)/shard_map/ppermute | solution.py:790
  3.8 3.5 %collective-permute-start.1 = (f32[8,32,128]{2,1,0:T(8,128)S(1)}, f32[8,32,128]{2,1,0:T(8,128)S(1)}, u32[]{:S(2)}, u32[]{:S(2)}) collective-permute-start(f32[8,32,128]{2,1,0:T(8,128)S(1)} %get-tuple-element.46), channel_id=1, source_target_pairs={{2,4},{4,2},{6,8},{8,6},{10,12},{12,10},{14,16},{16,14},{18,20},{2... | collective-permute-start | bytes 393224 | tf_op jit(solution)/shard_map/ppermute | solution.py:790
  7.3 0.7 %copy-start = (f32[2,2]{1,0:T(2,128)S(1)}, f32[2,2]{1,0:T(2,128)}, u32[]{:S(2)}) copy-start(f32[2,2]{1,0:T(2,128)} %param.5) | copy-start | bytes 52
  7.4 1.8 %collective-permute-start.2 = (f32[3,8,32,128]{3,2,1,0:T(8,128)S(1)}, f32[3,8,32,128]{3,2,1,0:T(8,128)S(1)}, u32[]{:S(2)}, u32[]{:S(2)}) collective-permute-start(f32[3,8,32,128]{3,2,1,0:T(8,128)S(1)} %pad_maximum_fusion.refs_1_), channel_id=1, source_target_pairs={{0,1},{1,0},{2,3},{3,2},{4,5},{5,4},{6,7},{7,6},{8,9},{9,8},{10,11... | collective-permute-start | bytes 1179656 | tf_op jit(solution)/shard_map/ppermute | solution.py:793

commit v3 on v2

--- a/solution.py
+++ b/solution.py
@@ -351,7 +351,7 @@
 
 def descend(sizes, ends, state, message_fields, message, first_rows):
     grids = sizes.grids
-    u, f, d, uc, rest = state
+    u, f, d, uc, (*rest, outgoing) = state
     (a0, z0), (a1, z1) = first_rows
     residual_strips(grids[0], ends, u[0], f[0], d[0], rest[0], a0, z0)
     restrict_first(grids, u[0], (u[1], uc[1]), 2, a1, z1)
@@ -369,8 +369,11 @@
         fields += [join_tiles(grids, d[2], (0, 2)), join_tiles(grids, d[2], (1, 1))]
     for place, tiles in enumerate(fields):
         for k, tile in enumerate(tiles):
-            for target in range(sizes.row_devices):
-                message[target, k, pl.ds(place * h, h), :] = tile[:h]
+            outgoing[pl.ds((k * message_fields + place) * h, h), :] = tile[:h]
+    targets, share, _ = message.shape
+    part = outgoing[pl.ds(lax.axis_index("gy") * share, share), :]
+    for target in range(targets):
+        message[target] = part
 
 
 def coarse_correction(sizes, fields):
@@ -798,7 +801,8 @@
         return pltpu.VMEM(shape, jnp.float32)
 
     def message_shape(fields):
-        return (row_devices, sizes.join_tiles, fields * sizes.join_rows, LANES)
+        share = sizes.join_tiles * fields * sizes.join_rows // column_devices
+        return (row_devices * column_devices, share, LANES)
 
     fields = [grid.shape(2) for grid in grids]
     datas = [grid.shape(3) for grid in grids]
@@ -807,6 +811,7 @@
         return shape[:2] + (shape[2] // 2,) + shape[3:]
 
     rests = [vmem(halved(fields[0])), vmem(fields[1]), vmem(fields[2])]
+    rests.append(vmem((sizes.join_tiles * 4 * sizes.join_rows, LANES)))
     join_whole = row_devices * sizes.join_rows
     coarse = [
         vmem((sizes.join_tiles, join_whole + 3 * SUB, LANES)),
@@ -832,12 +837,12 @@
     u0, u1, u2, f0, f1, f2, d0, d1, d2, uc1, uc2, message = call(
         start_kernel, outs, [vmem((sizes.tiles,) + tiles.shape[:3] + (2 * LANES,))] + rests
     )(spread, *pieces)
-    first_received = lax.all_to_all(message, "gx", 0, 0, tiled=True).reshape(-1, LANES)
+    first_received = lax.all_to_all(message, ("gx", "gy"), 0, 0, tiled=True).reshape(-1, LANES)
     outs = fields + fields[1:] + fields[1:] + [message_shape(2)]
     u0, u1, u2, f1, f2, uc1, uc2, message = call(middle_kernel, outs, coarse + rests)(
         first_received, u0, u1, u2, f0, f1, f2, d0, d1, d2, uc1, uc2
     )
-    received = lax.all_to_all(message, "gx", 0, 0, tiled=True).reshape(-1, LANES)
+    received = lax.all_to_all(message, ("gx", "gy"), 0, 0, tiled=True).reshape(-1, LANES)
     outs = [(2, slices, rows, columns)]
     return call(last_kernel, outs, [vmem(shape) for shape in fields] + coarse)(
         received, first_received, u0, u1, u2, f0, f1, f2, d0, d1, d2, uc1, uc2

time: 45.4 us -> 43.5 us (0.958)
  blocking collectives: 28.2 us -> 26.4 us
    all_to_all x2, blocking collectives: 28.2 us -> 26.4 us  [local(): lax.all_to_all(message, ('gx', 'gy'), 0, 0, tiled=True).reshape(-1, LANES)]
where the time goes in v3:
time: 43.5 us; the launch traced here: 43.3 us
  blocking collectives  26.4 us (61%)
  Pallas kernels  7.68 us (18%)
  waiting for transfers between devices  3.89 us (9%)
  starting transfers between devices  3.76 us (9%)
  other arithmetic  0.82 us (2%)
  local copies, waits for them, and re-layouts  0.72 us (2%)
    all_to_all x2, blocking collectives, local(): lax.all_to_all(message, ('gx', 'gy'), 0, 0, tiled=True).reshape(-1, LANES)  26.4 us
    ppermute x2, starting transfers between devices, local(): beside = [lax.ppermute(raw, 'gx', far), lax.ppermute(raw, 'gx', near)][::-1]  3.69 us
    pallas_call x1, Pallas kernels, local(): call(middle_kernel, outs, coarse + rests)  3.42 us
    ppermute x2, waiting for transfers between devices, local(): beside = [lax.ppermute(raw, 'gx', far), lax.ppermute(raw, 'gx', near)][::-1]  2.83 us
    pallas_call x1, Pallas kernels, local(): call(last_kernel, outs, [vmem(shape) for shape in fields] + coarse)  2.71 us
    pallas_call x1, Pallas kernels, local(): call(start_kernel, outs, [vmem((sizes.tiles,) + tiles.shape[:3] + (2 * LA...  1.55 us
    ppermute x1, waiting for transfers between devices, local(): pieces = (tiles, lax.ppermute(tiles, 'gy', [(0, 1), (1, 0)]))  1.06 us
  transfers between devices with their start and end apart: 3, of which 2 were waited for; matrix products, arithmetic and copies ran while one was open for 0% of the time, Pallas kernels for 0%

profile of v3, /device:TPU:0, one launch (start us, length us, event | category | flops | bytes accessed | tf_op | source)
XLA Modules:
  0.0 43.3 jit_solution(7945517490479916579)
XLA Ops:
  0.0 0.8 %fusion = (f32[1,8,32,128]{3,2,1,0:T(8,128)S(1)}, f32[8,32,128]{2,1,0:T(8,128)S(1)}) fusion(bf16[4,32,128]{2,1,0:T(8,128)(2,1)} %bitcast.13, bf16[4,32,128]{2,1,0:T(8,128)(2,1)} %bitcast.14), kind=kLoop, calls=%fused_computation.2 | loop fusion | flops 65536 | bytes 327680 | tf_op jit(solution)/shard_map/stack | solution.py:794
  0.8 3.0 %collective-permute-start = (f32[8,32,128]{2,1,0:T(8,128)S(1)}, f32[8,32,128]{2,1,0:T(8,128)S(1)}, u32[]{:S(2)}, u32[]{:S(2)}) collective-permute-start(f32[8,32,128]{2,1,0:T(8,128)S(1)} %get-tuple-element.46), channel_id=1, source_target_pairs={{0,2},{2,0},{4,6},{6,4},{8,10},{10,8},{12,14},{14,12},{16,18},{18,... | collective-permute-start | bytes 393224 | tf_op jit(solution)/shard_map/ppermute | solution.py:793
  3.8 0.7 %collective-permute-start.1 = (f32[8,32,128]{2,1,0:T(8,128)S(1)}, f32[8,32,128]{2,1,0:T(8,128)S(1)}, u32[]{:S(2)}, u32[]{:S(2)}) collective-permute-start(f32[8,32,128]{2,1,0:T(8,128)S(1)} %get-tuple-element.46), channel_id=1, source_target_pairs={{2,4},{4,2},{6,8},{8,6},{10,12},{12,10},{14,16},{16,14},{18,20},{2... | collective-permute-start | bytes 393224 | tf_op jit(solution)/shard_map/ppermute | solution.py:793
  4.5 2.8 %collective-permute-done = f32[8,32,128]{2,1,0:T(8,128)S(1)} collective-permute-done((f32[8,32,128]{2,1,0:T(8,128)S(1)}, f32[8,32,128]{2,1,0:T(8,128)S(1)}, u32[]{:S(2)}, u32[]{:S(2)}) %collective-permute-start) | collective-permute-done | bytes 131104 | tf_op jit(solution)/shard_map/ppermute | solution.py:793
  7.3 0.0 collective-permute-done.1
  7.3 0.0 copy-start
  7.4 0.1 collective-permute-start.2
  7.4 0.6 %copy-done = f32[2,2]{1,0:T(2,128)S(1)} copy-done((f32[2,2]{1,0:T(2,128)S(1)}, f32[2,2]{1,0:T(2,128)}, u32[]{:S(2)}) %copy-start) | copy-done | bytes 40
  8.0 0.1 broadcast_in_dim.7
  8.1 1.1 %collective-permute-done.2.refs_2_ = f32[3,8,32,128]{3,2,1,0:T(8,128)S(1)} collective-permute-done((f32[3,8,32,128]{3,2,1,0:T(8,128)S(1)}, f32[3,8,32,128]{3,2,1,0:T(8,128)S(1)}, u32[]{:S(2)}, u32[]{:S(2)}) %collective-permute-start.2) | collective-permute-done | bytes 393248 | tf_op jit(solution)/shard_map/ppermute | solution.py:796
  9.2 0.1 broadcast_in_dim.8.refs_0_
  9.2 1.6 %start_kernel.1 = (f32[2,2,2,104,128]{4,3,2,1,0:T(8,128)S(1)}, f32[2,2,1,56,128]{4,3,2,1,0:T(8,128)S(1)}, f32[1,2,1,32,128]{4,3,2,1,0:T(8,128)S(1)}, f32[2,2,2,1...) custom-call(f32[4,8,128]{2,1,0:T(8,128)S(1)} %broadcast_in_dim.8.ref, ...), custom_call_target="tpu_custom_call" | custom-call | tf_op jit(solution)/shard_map/start_kernel/pallas_call | solution.py:837
  10.8 17.2 %all_to_all.10 = f32[32,8,128]{2,1,0:T(8,128)S(1)} all-to-all(f32[32,8,128]{2,1,0:T(8,128)S(1)} %get-tuple-element.25), channel_id=1, replica_groups=mesh['gx'=16,'gy'=2] {'gx','gy'}, dimensions={0} | all-to-all | bytes 262144 | tf_op jit(solution)/shard_map/all_to_all | solution.py:840
  28.0 3.4 %middle_kernel.1 = (f32[2,2,2,104,128]{4,3,2,1,0:T(8,128)S(1)}, f32[2,2,1,56,128]{4,3,2,1,0:T(8,128)S(1)}, f32[1,2,1,32,128]{4,3,2,1,0:T(8,128)S(1)}, f32[2,2,1,...) custom-call(f32[256,128]{1,0:T(8,128)S(1)} %bitcast.8, ...), custom_call_target="tpu_custom_call" | custom-call | tf_op jit(solution)/shard_map/middle_kernel/pallas_call | solution.py:842
  31.4 9.2 %all_to_all.11 = f32[32,4,128]{2,1,0:T(4,128)S(1)} all-to-all(f32[32,4,128]{2,1,0:T(4,128)S(1)} %get-tuple-element.37), channel_id=1, replica_groups=mesh['gx'=16,'gy'=2] {'gx','gy'}, dimensions={0} | all-to-all | bytes 131072 | tf_op jit(solution)/shard_map/all_to_all | solution.py:845
  40.6 2.7 %last_kernel.1 = f32[2,2,32,128]{3,2,1,0:T(8,128)} custom-call(f32[128,128]{1,0:T(8,128)S(1)} %bitcast.10, f32[256,128]{1,0:T(8,128)S(1)} %bitcast.9, f32[2,2,2,104,128]{4,3,2,1,0:T(8,128)S(1)} %get-tuple-element.38.refs_2_, f32[2,2,1,56,128]{4,3,2,1,0:T(8,128)S(1)} %get-tuple-element.39.refs_3_, f32[1,2,1,32,128]{4,3,2,1,0:T(8,128)S(1)} %get-tuple-element.40.refs_4_, ...), custom_call_target="tpu_custom_call" | custom-call | tf_op jit(solution)/shard_map/last_kernel/pallas_call | solution.py:847
  (1 shorter events, 0.0 us)
Async XLA Ops:
  0.8 6.5 %collective-permute-start = (f32[8,32,128]{2,1,0:T(8,128)S(1)}, f32[8,32,128]{2,1,0:T(8,128)S(1)}, u32[]{:S(2)}, u32[]{:S(2)}) collective-permute-start(f32[8,32,128]{2,1,0:T(8,128)S(1)} %get-tuple-element.46), channel_id=1, source_target_pairs={{0,2},{2,0},{4,6},{6,4},{8,10},{10,8},{12,14},{14,12},{16,18},{18,... | collective-permute-start | bytes 393224 | tf_op jit(solution)/shard_map/ppermute | solution.py:793
  3.8 3.5 %collective-permute-start.1 = (f32[8,32,128]{2,1,0:T(8,128)S(1)}, f32[8,32,128]{2,1,0:T(8,128)S(1)}, u32[]{:S(2)}, u32[]{:S(2)}) collective-permute-start(f32[8,32,128]{2,1,0:T(8,128)S(1)} %get-tuple-element.46), channel_id=1, source_target_pairs={{2,4},{4,2},{6,8},{8,6},{10,12},{12,10},{14,16},{16,14},{18,20},{2... | collective-permute-start | bytes 393224 | tf_op jit(solution)/shard_map/ppermute | solution.py:793
  7.3 0.7 %copy-start = (f32[2,2]{1,0:T(2,128)S(1)}, f32[2,2]{1,0:T(2,128)}, u32[]{:S(2)}) copy-start(f32[2,2]{1,0:T(2,128)} %param.5) | copy-start | bytes 52
  7.4 1.8 %collective-permute-start.2 = (f32[3,8,32,128]{3,2,1,0:T(8,128)S(1)}, f32[3,8,32,128]{3,2,1,0:T(8,128)S(1)}, u32[]{:S(2)}, u32[]{:S(2)}) collective-permute-start(f32[3,8,32,128]{3,2,1,0:T(8,128)S(1)} %pad_maximum_fusion.refs_1_), channel_id=1, source_target_pairs={{0,1},{1,0},{2,3},{3,2},{4,5},{5,4},{6,7},{7,6},{8,9},{9,8},{10,11... | collective-permute-start | bytes 1179656 | tf_op jit(solution)/shard_map/ppermute | solution.py:796

commit v4 on v3

--- a/solution.py
+++ b/solution.py
@@ -339,17 +339,15 @@
                     target[0, member, tile, pl.ds(start, SUB), :] = merged
 
 
-def join_tiles(grids, ref, members):
+def join_tiles(grids, ref, start):
     grid = grids[2]
     flat = [
-        pair_rows(ref, 0, member, tile, grid.own // 2)
-        for member in members
-        for tile in range(grid.tiles)
+        pair_rows(ref, 0, member, tile, start) for member in range(2) for tile in range(grid.tiles)
     ]
     return [0.25 * merge_pair(flat[2 * k], flat[2 * k + 1]) for k in range(len(flat) // 2)]
 
 
-def descend(sizes, ends, state, message_fields, message, first_rows):
+def descend(sizes, ends, state, weights, message, first_rows):
     grids = sizes.grids
     u, f, d, uc, (*rest, outgoing) = state
     (a0, z0), (a1, z1) = first_rows
@@ -364,19 +362,21 @@
     first_relax_strips(grids[2], ends, u[2], f[2], d[2], 0, strips)
     residual_strips(grids[2], ends, u[2], f[2], d[2], rest[2], 0, strips)
     h = sizes.join_rows
-    fields = [join_tiles(grids, u[2], (0, 1)), join_tiles(grids, rest[2], (0, 1))]
-    if message_fields == 4:
-        fields += [join_tiles(grids, d[2], (0, 2)), join_tiles(grids, d[2], (1, 1))]
+    fields = [join_tiles(grids, ref, grids[2].own // 2) for ref in (u[2], rest[2])]
+    if weights is not None:
+        fields.append(weights)
     for place, tiles in enumerate(fields):
         for k, tile in enumerate(tiles):
-            outgoing[pl.ds((k * message_fields + place) * h, h), :] = tile[:h]
-    targets, share, _ = message.shape
-    part = outgoing[pl.ds(lax.axis_index("gy") * share, share), :]
-    for target in range(targets):
-        message[target] = part
-
-
-def coarse_correction(sizes, fields):
+            outgoing[pl.ds((k * len(fields) + place) * h, h), :] = tile[:h]
+    targets, parts, share, _ = message.shape
+    base = lax.axis_index("gy") * (parts * share)
+    for place in range(parts):
+        part = outgoing[pl.ds(base + place * share, share), :]
+        for target in range(targets):
+            message[target, place] = part
+
+
+def coarse_correction(sizes, mixing, fields):
     tiles = max(1, sizes.join_tiles // 2)
     width = sizes.join_width
     lane, row = lane_of(), row_of()
@@ -418,11 +418,17 @@
     def subtract(first, second):
         return each(lambda a, b: a - b, first, second)
 
-    estimate, rest, diagonal, cross = fields
-    matrices = [(*split(diagonal), cross[:tiles])]
-    for level in range(JOIN + 1, LEVELS):
-        step = 1 << (level - JOIN - 1)
-        matrices.append(tuple(mean(part, step) for part in matrices[-1]))
+    estimate, rest, weights = fields
+    _, *factors = normal_factors(mixing)
+    means = split(weights)
+    matrices = []
+    for level in range(JOIN, LEVELS):
+        if level > JOIN:
+            means = [mean(part, 1 << (level - JOIN - 1)) for part in means]
+        water, cross, bone = (
+            each(lambda a, b, pair=pair: a * pair[0] + b * pair[1], *means) for pair in factors
+        )
+        matrices.append((water, bone, cross))
 
     def sums(level, values, with_factor):
         step = 1 << (level - JOIN)
@@ -510,7 +516,7 @@
     return join(*cycle(JOIN, split(estimate), split(rest)))
 
 
-def ascend(sizes, ends, row_index, received, state, scratch, level_rows):
+def ascend(sizes, ends, row_index, mixing, received, state, scratch, level_rows):
     grids = sizes.grids
     u, f, d, uc = state
     correction, raised = scratch
@@ -536,7 +542,7 @@
                 for k in range(sizes.join_tiles)
             ]
         )
-    values = coarse_correction(sizes, fields)
+    values = coarse_correction(sizes, mixing, fields)
     for k in range(sizes.join_tiles):
         correction[k, :SUB, :] = jnp.zeros((SUB, LANES), jnp.float32)
         correction[k, pl.ds(SUB + whole, 2 * SUB), :] = jnp.zeros((2 * SUB, LANES), jnp.float32)
@@ -611,6 +617,14 @@
     return row_index, (row_index > 0, row_index < sizes.row_devices - 1)
 
 
+def normal_factors(mixing):
+    m = [[mixing[2 * i + j] for j in range(2)] for i in range(2)]
+    water = [m[0][0] * m[0][0], m[1][0] * m[1][0]]
+    cross = [m[0][0] * m[0][1], m[1][0] * m[1][1]]
+    bone = [m[0][1] * m[0][1], m[1][1] * m[1][1]]
+    return m, water, cross, bone
+
+
 def split_columns(sizes, pieces, swapped, out):
     shape = (2 * LANES, 2 * LANES)
     source, target = row_of(shape), lane_of(shape)
@@ -633,16 +647,13 @@
     else:
         pieces, refs = [refs[0].at[k] for k in range(sizes.column_devices)], refs[1:]
         swapped = 0
-    u0, u1, u2, f0, f1, f2, d0, d1, d2, uc1, uc2, message, ordered, *rest = refs
+    u0, u1, u2, f0, f1, f2, d0, d1, d2, uc1, uc2, message, ordered, w0, w1, w2, *rest = refs
     split_columns(sizes, pieces, swapped, ordered)
     grids = sizes.grids
     row_index, ends = domain_ends(sizes)
     for grid, ref in zip(grids, (u0, u1, u2)):
         zero_margin(grid, ref)
-    m = [[mixing[2 * i + j] for j in range(2)] for i in range(2)]
-    water = [m[0][0] * m[0][0], m[1][0] * m[1][0]]
-    cross = [m[0][0] * m[0][1], m[1][0] * m[1][1]]
-    bone = [m[0][1] * m[0][1], m[1][1] * m[1][1]]
+    m, water, cross, bone = normal_factors(mixing)
     odd_device = row_index % 2
     parts = (2 - odd_device, 0, 1 + odd_device)
     beyond = (
@@ -679,6 +690,9 @@
             for tile in range(half):
                 counts = [load(0, energy, tile) for energy in range(2)]
                 weights = [load(1, energy, tile) for energy in range(2)]
+                if part == 1:
+                    for energy, pair in enumerate(weights):
+                        w0[group, energy, tile, pl.ds(inner, SUB), :] = pair[0] + pair[1]
                 for parity in range(2):
                     y = [counts[energy][parity] for energy in range(2)]
                     w = [weights[energy][parity] for energy in range(2)]
@@ -707,7 +721,9 @@
     restrict_second(grids, d1, (d2,), 3, 0, grids[2].rows // SUB)
     state = ((u0, u1, u2), (f0, f1, f2), (d0, d1, d2), (None, uc1, uc2), rest)
     all_rows = ((0, grids[0].rows // SUB), (0, grids[1].rows // SUB))
-    descend(sizes, ends, state, 4, message, all_rows)
+    restrict_first(grids, w0, (w1,), 2, 0, grids[1].own // SUB, summed=True)
+    restrict_second(grids, w1, (w2,), 2, 0, grids[2].own // SUB)
+    descend(sizes, ends, state, join_tiles(grids, w2, 0), message, all_rows)
 
 
 def middle_rows(sizes):
@@ -718,7 +734,7 @@
 
 
 def middle_kernel(
-    sizes, received, u0i, u1i, u2i, f0, f1i, f2i, d0, d1, d2, uc1i, uc2i,
+    sizes, mixing, received, u0i, u1i, u2i, f0, f1i, f2i, d0, d1, d2, uc1i, uc2i,
     u0, u1, u2, f1, f2, uc1, uc2, message,
     correction, raised0, raised1, raised2, *rest,
 ):
@@ -727,20 +743,20 @@
     for source, target in ((u0i, u0), (u1i, u1), (u2i, u2)):
         target[...] = source[...]
     scratch = (correction, (raised0, raised1, raised2))
-    fields = [(received, k, 4) for k in range(4)]
+    fields = [(received, k, 3) for k in range(3)]
     span = middle_rows(sizes)
     state = ((u0, u1, u2), (f0, f1i, f2i), (d0, d1, d2), (None, uc1i, uc2i))
-    ascend(sizes, ends, row_index, fields, state, scratch, span)
+    ascend(sizes, ends, row_index, mixing, fields, state, scratch, span)
     (a0, z0), _ = span
     relax_strips(grids[0], ends, u0, f0, d0, a0, z0)
     zero_margin(grids[1], u1)
     zero_margin(grids[2], u2)
     state = ((u0, u1, u2), (f0, f1, f2), (d0, d1, d2), (None, uc1, uc2), rest)
-    descend(sizes, ends, state, 2, message, span)
+    descend(sizes, ends, state, None, message, span)
 
 
 def last_kernel(
-    sizes, received, first_received, u0, u1, u2, f0, f1, f2, d0, d1, d2, uc1, uc2,
+    sizes, mixing, received, first_received, u0, u1, u2, f0, f1, f2, d0, d1, d2, uc1, uc2,
     out,
     v0, v1, v2, correction, raised0, raised1, raised2,
 ):
@@ -749,11 +765,11 @@
     for source, target in ((u0, v0), (u1, v1), (u2, v2)):
         target[...] = source[...]
     scratch = (correction, (raised0, raised1, raised2))
-    fields = [(received, k, 2) for k in range(2)] + [(first_received, k, 4) for k in (2, 3)]
+    fields = [(received, 0, 2), (received, 1, 2), (first_received, 2, 3)]
     own = (sizes.rows // SUB, 2 * sizes.rows // SUB)
     span = (own, middle_rows(sizes)[1])
     state = ((v0, v1, v2), (f0, f1, f2), (d0, d1, d2), (None, uc1, uc2))
-    ascend(sizes, ends, row_index, fields, state, scratch, span)
+    ascend(sizes, ends, row_index, mixing, fields, state, scratch, span)
     column_index = lax.axis_index("gy")
     lane = lane_of()
     tile = column_index // 2
@@ -802,7 +818,8 @@
 
     def message_shape(fields):
         share = sizes.join_tiles * fields * sizes.join_rows // column_devices
-        return (row_devices * column_devices, share, LANES)
+        group = next(g for g in (8, 4, 2, 1) if share % g == 0)
+        return (row_devices * column_devices, share // group, group, LANES)
 
     fields = [grid.shape(2) for grid in grids]
     datas = [grid.shape(3) for grid in grids]
@@ -811,7 +828,7 @@
         return shape[:2] + (shape[2] // 2,) + shape[3:]
 
     rests = [vmem(halved(fields[0])), vmem(fields[1]), vmem(fields[2])]
-    rests.append(vmem((sizes.join_tiles * 4 * sizes.join_rows, LANES)))
+    rests.append(vmem((sizes.join_tiles * 3 * sizes.join_rows, LANES)))
     join_whole = row_devices * sizes.join_rows
     coarse = [
         vmem((sizes.join_tiles, join_whole + 3 * SUB, LANES)),
@@ -832,20 +849,25 @@
             compiler_params=pltpu.CompilerParams(vmem_limit_bytes=vmem_limit),
         )
 
-    outs = fields + fields + datas + fields[1:] + [message_shape(4)]
+    outs = fields + fields + datas + fields[1:] + [message_shape(3)]
+    weights = [
+        vmem((slices, 2, sizes.tiles, rows, LANES)),
+        vmem((slices, 2, sizes.tiles, grids[1].own, LANES)),
+        vmem((1, 2, grids[2].tiles, max(grids[2].own, 2 * SUB), LANES)),
+    ]
     spread = jnp.broadcast_to(mixing.reshape(-1, 1, 1), (mixing.size, SUB, LANES))
     u0, u1, u2, f0, f1, f2, d0, d1, d2, uc1, uc2, message = call(
-        start_kernel, outs, [vmem((sizes.tiles,) + tiles.shape[:3] + (2 * LANES,))] + rests
+        start_kernel, outs, [vmem((sizes.tiles,) + tiles.shape[:3] + (2 * LANES,))] + weights + rests
     )(spread, *pieces)
     first_received = lax.all_to_all(message, ("gx", "gy"), 0, 0, tiled=True).reshape(-1, LANES)
     outs = fields + fields[1:] + fields[1:] + [message_shape(2)]
     u0, u1, u2, f1, f2, uc1, uc2, message = call(middle_kernel, outs, coarse + rests)(
-        first_received, u0, u1, u2, f0, f1, f2, d0, d1, d2, uc1, uc2
+        spread, first_received, u0, u1, u2, f0, f1, f2, d0, d1, d2, uc1, uc2
     )
     received = lax.all_to_all(message, ("gx", "gy"), 0, 0, tiled=True).reshape(-1, LANES)
     outs = [(2, slices, rows, columns)]
     return call(last_kernel, outs, [vmem(shape) for shape in fields] + coarse)(
-        received, first_received, u0, u1, u2, f0, f1, f2, d0, d1, d2, uc1, uc2
+        spread, received, first_received, u0, u1, u2, f0, f1, f2, d0, d1, d2, uc1, uc2
     )[0]
 
 

time: 43.5 us -> 43.1 us (level)
  blocking collectives: 26.4 us -> 25.9 us
    all_to_all x2, blocking collectives: 26.4 us -> 25.9 us  [local(): lax.all_to_all(message, ('gx', 'gy'), 0, 0, tiled=True).reshape(-1, LANES)]
where the time goes in v4:
time: 43.1 us; the launch traced here: 42.8 us
  blocking collectives  25.9 us (60%)
  Pallas kernels  7.73 us (18%)
  waiting for transfers between devices  3.89 us (9%)
  starting transfers between devices  3.76 us (9%)
  other arithmetic  0.82 us (2%)
  local copies, waits for them, and re-layouts  0.72 us (2%)
    all_to_all x2, blocking collectives, local(): lax.all_to_all(message, ('gx', 'gy'), 0, 0, tiled=True).reshape(-1, LANES)  25.9 us
    ppermute x2, starting transfers between devices, local(): beside = [lax.ppermute(raw, 'gx', far), lax.ppermute(raw, 'gx', near)][::-1]  3.69 us
    pallas_call x1, Pallas kernels, local(): call(middle_kernel, outs, coarse + rests)  3.43 us
    ppermute x2, waiting for transfers between devices, local(): beside = [lax.ppermute(raw, 'gx', far), lax.ppermute(raw, 'gx', near)][::-1]  2.83 us
    pallas_call x1, Pallas kernels, local(): call(last_kernel, outs, [vmem(shape) for shape in fields] + coarse)  2.72 us
    pallas_call x1, Pallas kernels, local(): call(start_kernel, outs, [vmem((sizes.tiles,) + tiles.shape[:3] + (2 * LA...  1.58 us
    ppermute x1, waiting for transfers between devices, local(): pieces = (tiles, lax.ppermute(tiles, 'gy', [(0, 1), (1, 0)]))  1.06 us
  transfers between devices with their start and end apart: 3, of which 2 were waited for; matrix products, arithmetic and copies ran while one was open for 0% of the time, Pallas kernels for 0%

profile of v4, /device:TPU:0, one launch (start us, length us, event | category | flops | bytes accessed | tf_op | source)
XLA Modules:
  0.0 42.8 jit_solution(8906663398195461015)
XLA Ops:
  0.0 0.8 %fusion = (f32[1,8,32,128]{3,2,1,0:T(8,128)S(1)}, f32[8,32,128]{2,1,0:T(8,128)S(1)}) fusion(bf16[4,32,128]{2,1,0:T(8,128)(2,1)} %bitcast.13, bf16[4,32,128]{2,1,0:T(8,128)(2,1)} %bitcast.14), kind=kLoop, calls=%fused_computation.2 | loop fusion | flops 65536 | bytes 327680 | tf_op jit(solution)/shard_map/stack | solution.py:810
  0.8 3.0 %collective-permute-start = (f32[8,32,128]{2,1,0:T(8,128)S(1)}, f32[8,32,128]{2,1,0:T(8,128)S(1)}, u32[]{:S(2)}, u32[]{:S(2)}) collective-permute-start(f32[8,32,128]{2,1,0:T(8,128)S(1)} %get-tuple-element.46), channel_id=1, source_target_pairs={{0,2},{2,0},{4,6},{6,4},{8,10},{10,8},{12,14},{14,12},{16,18},{18,... | collective-permute-start | bytes 393224 | tf_op jit(solution)/shard_map/ppermute | solution.py:809
  3.8 0.7 %collective-permute-start.1 = (f32[8,32,128]{2,1,0:T(8,128)S(1)}, f32[8,32,128]{2,1,0:T(8,128)S(1)}, u32[]{:S(2)}, u32[]{:S(2)}) collective-permute-start(f32[8,32,128]{2,1,0:T(8,128)S(1)} %get-tuple-element.46), channel_id=1, source_target_pairs={{2,4},{4,2},{6,8},{8,6},{10,12},{12,10},{14,16},{16,14},{18,20},{2... | collective-permute-start | bytes 393224 | tf_op jit(solution)/shard_map/ppermute | solution.py:809
  4.5 2.8 %collective-permute-done = f32[8,32,128]{2,1,0:T(8,128)S(1)} collective-permute-done((f32[8,32,128]{2,1,0:T(8,128)S(1)}, f32[8,32,128]{2,1,0:T(8,128)S(1)}, u32[]{:S(2)}, u32[]{:S(2)}) %collective-permute-start) | collective-permute-done | bytes 131104 | tf_op jit(solution)/shard_map/ppermute | solution.py:809
  7.3 0.0 collective-permute-done.1
  7.3 0.0 copy-start
  7.4 0.1 collective-permute-start.2
  7.4 0.6 %copy-done = f32[2,2]{1,0:T(2,128)S(1)} copy-done((f32[2,2]{1,0:T(2,128)S(1)}, f32[2,2]{1,0:T(2,128)}, u32[]{:S(2)}) %copy-start) | copy-done | bytes 40
  8.0 0.1 broadcast_in_dim.7
  8.1 1.1 %collective-permute-done.2.refs_2_ = f32[3,8,32,128]{3,2,1,0:T(8,128)S(1)} collective-permute-done((f32[3,8,32,128]{3,2,1,0:T(8,128)S(1)}, f32[3,8,32,128]{3,2,1,0:T(8,128)S(1)}, u32[]{:S(2)}, u32[]{:S(2)}) %collective-permute-start.2) | collective-permute-done | bytes 393248 | tf_op jit(solution)/shard_map/ppermute | solution.py:812
  9.2 0.1 broadcast_in_dim.8.refs_0_
  9.2 1.6 %start_kernel.1 = (f32[2,2,2,104,128]{4,3,2,1,0:T(8,128)S(1)}, f32[2,2,1,56,128]{4,3,2,1,0:T(8,128)S(1)}, f32[1,2,1,32,128]{4,3,2,1,0:T(8,128)S(1)}, f32[2,2,2,1...) custom-call(f32[4,8,128]{2,1,0:T(8,128)S(1)} %broadcast_in_dim.8.ref, ...), custom_call_target="tpu_custom_call" | custom-call | tf_op jit(solution)/shard_map/start_kernel/pallas_call | solution.py:859
  10.8 16.8 %all_to_all.10 = f32[32,3,2,128]{3,2,1,0:T(2,128)S(1)} all-to-all(f32[32,3,2,128]{3,2,1,0:T(2,128)S(1)} %get-tuple-element.25), channel_id=1, replica_groups=mesh['gx'=16,'gy'=2] {'gx','gy'}, dimensions={0} | all-to-all | bytes 196608 | tf_op jit(solution)/shard_map/all_to_all | solution.py:862
  27.6 3.4 %middle_kernel.1 = (f32[2,2,2,104,128]{4,3,2,1,0:T(8,128)S(1)}, f32[2,2,1,56,128]{4,3,2,1,0:T(8,128)S(1)}, f32[1,2,1,32,128]{4,3,2,1,0:T(8,128)S(1)}, f32[2,2,1,...) custom-call(f32[4,8,128]{2,1,0:T(8,128)S(1)} %broadcast_in_dim.8.ref, ...), custom_call_target="tpu_custom_call" | custom-call | tf_op jit(solution)/shard_map/middle_kernel/pallas_call | solution.py:864
  31.0 9.1 %all_to_all.11 = f32[32,1,4,128]{3,2,1,0:T(4,128)S(1)} all-to-all(f32[32,1,4,128]{3,2,1,0:T(4,128)S(1)} %get-tuple-element.37), channel_id=1, replica_groups=mesh['gx'=16,'gy'=2] {'gx','gy'}, dimensions={0} | all-to-all | bytes 131072 | tf_op jit(solution)/shard_map/all_to_all | solution.py:867
  40.1 2.7 %last_kernel.1 = f32[2,2,32,128]{3,2,1,0:T(8,128)} custom-call(f32[4,8,128]{2,1,0:T(8,128)S(1)} %broadcast_in_dim.8.refs_0_, f32[128,128]{1,0:T(8,128)S(1)} %bitcast.10, f32[192,128]{1,0:T(8,128)S(1)} %bitcast.9, f32[2,2,2,104,128]{4,3,2,1,0:T(8,128)S(1)} %get-tuple-element.38.refs_3_, f32[2,2,1,56,128]{4,3,2,1,0:T(8,128)S(1)} %get-tuple-element.39.refs_4_, ...), custom_call_target="tpu_custom_call" | custom-call | tf_op jit(solution)/shard_map/last_kernel/pallas_call | solution.py:869
  (1 shorter events, 0.0 us)
Async XLA Ops:
  0.8 6.5 %collective-permute-start = (f32[8,32,128]{2,1,0:T(8,128)S(1)}, f32[8,32,128]{2,1,0:T(8,128)S(1)}, u32[]{:S(2)}, u32[]{:S(2)}) collective-permute-start(f32[8,32,128]{2,1,0:T(8,128)S(1)} %get-tuple-element.46), channel_id=1, source_target_pairs={{0,2},{2,0},{4,6},{6,4},{8,10},{10,8},{12,14},{14,12},{16,18},{18,... | collective-permute-start | bytes 393224 | tf_op jit(solution)/shard_map/ppermute | solution.py:809
  3.8 3.5 %collective-permute-start.1 = (f32[8,32,128]{2,1,0:T(8,128)S(1)}, f32[8,32,128]{2,1,0:T(8,128)S(1)}, u32[]{:S(2)}, u32[]{:S(2)}) collective-permute-start(f32[8,32,128]{2,1,0:T(8,128)S(1)} %get-tuple-element.46), channel_id=1, source_target_pairs={{2,4},{4,2},{6,8},{8,6},{10,12},{12,10},{14,16},{16,14},{18,20},{2... | collective-permute-start | bytes 393224 | tf_op jit(solution)/shard_map/ppermute | solution.py:809
  7.3 0.7 %copy-start = (f32[2,2]{1,0:T(2,128)S(1)}, f32[2,2]{1,0:T(2,128)}, u32[]{:S(2)}) copy-start(f32[2,2]{1,0:T(2,128)} %param.5) | copy-start | bytes 52
  7.4 1.8 %collective-permute-start.2 = (f32[3,8,32,128]{3,2,1,0:T(8,128)S(1)}, f32[3,8,32,128]{3,2,1,0:T(8,128)S(1)}, u32[]{:S(2)}, u32[]{:S(2)}) collective-permute-start(f32[3,8,32,128]{3,2,1,0:T(8,128)S(1)} %pad_maximum_fusion.refs_1_), channel_id=1, source_target_pairs={{0,1},{1,0},{2,3},{3,2},{4,5},{5,4},{6,7},{7,6},{8,9},{9,8},{10,11... | collective-permute-start | bytes 1179656 | tf_op jit(solution)/shard_map/ppermute | solution.py:812

commit v5 on v4

--- a/solution.py
+++ b/solution.py
@@ -164,6 +164,7 @@
         self.join_rows = rows >> JOIN
         self.join_tiles = slices * self.tiles // 2
         self.join_width = self.tiles * LANES >> (JOIN - 1)
+        self.join_halves = 2 if self.join_tiles == 1 else 1
         self.grids = [Grid(level, self) for level in range(JOIN)]
 
 
@@ -388,19 +389,21 @@
             for k in range(tiles)
         ]
 
+    cut = sizes.join_halves == 2
+
+    def exchange(first, second):
+        pairs = list(zip(first, second))
+        low_lanes = [jnp.where(low, a, roll_lanes(b, LANES // 2)) for a, b in pairs]
+        return low_lanes, [jnp.where(low, roll_lanes(a, LANES // 2), b) for a, b in pairs]
+
     def split(values):
-        if sizes.join_tiles > 1:
+        if not cut:
             return values[:tiles], values[tiles:]
-        other = each(lambda x: roll_lanes(x, LANES // 2), values)
-        return (
-            each(lambda x, y: jnp.where(low, x, y), values, other),
-            each(lambda x, y: jnp.where(low, y, x), values, other),
-        )
+        first, second = exchange(*values)
+        return [first], [second]
 
     def join(first, second):
-        if sizes.join_tiles > 1:
-            return first + second
-        return each(lambda x, y: jnp.where(low, x, y), first, second)
+        return list(exchange(first[0], second[0])) if cut else first + second
 
     def mean(values, step):
         pair = (lane & step) == 0
@@ -447,16 +450,23 @@
             edges = [
                 flux(b - a, with_factor) for a, b in zip(value, value[1:])
             ]
-            first = flux(roll_rows(value[-1], 1) - value[0], with_factor)
-            last = flux(roll_rows(value[0], -1) - value[-1], with_factor)
+            above, below = roll_rows(value[-1], 1), roll_rows(value[0], -1)
+            has_above, has_below = row > 0, row < SUB - 1
+            if cut:
+                above = jnp.where(has_above, above, roll_lanes(above, LANES // 2))
+                below = jnp.where(has_below, below, roll_lanes(below, LANES // 2))
+                has_above = jnp.logical_or(has_above, jnp.logical_not(low))
+                has_below = jnp.logical_or(has_below, low)
+            first = flux(above - value[0], with_factor)
+            last = flux(below - value[-1], with_factor)
             for place in range(2 if with_factor else 1):
                 total = totals[place][k]
                 for v, edge in enumerate(edges):
                     total[v] = total[v] + edge[place]
                     opposite = edge[place] if place else -edge[place]
                     total[v + 1] = total[v + 1] + opposite
-                total[0] = total[0] + keep(row > 0, first[place])
-                total[-1] = total[-1] + keep(row < SUB - 1, last[place])
+                total[0] = total[0] + keep(has_above, first[place])
+                total[-1] = total[-1] + keep(has_below, last[place])
         return totals
 
     def apply(level, values, flows, with_factor):
@@ -518,36 +528,30 @@
 
 def ascend(sizes, ends, row_index, mixing, received, state, scratch, level_rows):
     grids = sizes.grids
-    u, f, d, uc = state
+    old, u, f, d, uc = state
     correction, raised = scratch
     h = sizes.join_rows
     whole = sizes.row_devices * h
-    count = whole // SUB
+    halves = sizes.join_halves
+    count = whole // SUB // halves
+    places = [(k, half) for k in range(sizes.join_tiles) for half in range(halves)]
     fields = []
     for ref, field, total in received:
         block = sizes.join_tiles * total * h
-        fields.append(
-            [
-                [
-                    ref[
-                        pl.ds(
-                            v // h * block + (k * total + field) * h + v % h,
-                            SUB,
-                            stride=count // h * block,
-                        ),
-                        :,
-                    ]
-                    for v in range(count)
-                ]
-                for k in range(sizes.join_tiles)
-            ]
-        )
+
+        def rows_of(k, half, v):
+            start = (half * count * SUB + v) // h * block + (k * total + field) * h + v % h
+            return ref[pl.ds(start, SUB, stride=count // h * block), :]
+
+        fields.append([[rows_of(k, half, v) for v in range(count)] for k, half in places])
     values = coarse_correction(sizes, mixing, fields)
     for k in range(sizes.join_tiles):
         correction[k, :SUB, :] = jnp.zeros((SUB, LANES), jnp.float32)
         correction[k, pl.ds(SUB + whole, 2 * SUB), :] = jnp.zeros((2 * SUB, LANES), jnp.float32)
+    for (k, half), lines in zip(places, values):
         for v in range(count):
-            correction[k, pl.ds(SUB + v, SUB, stride=count), :] = values[k][v]
+            rows = pl.ds(SUB + half * count * SUB + v, SUB, stride=count)
+            correction[k, rows, :] = lines[v]
 
     grid = grids[2]
     strips = grid.rows // SUB
@@ -559,7 +563,7 @@
                 member, tile = divmod(2 * k + side, grid.tiles)
                 for odd in range(2):
                     raised[2][0, member, tile, pl.ds(2 * start + odd, SUB, stride=2), :] = part
-    add_raised(grid, u[2], raised[2], 0, strips)
+    add_raised(grid, old[2], u[2], raised[2], 0, strips)
     relax_strips(grid, ends, u[2], f[2], d[2], 0, strips)
 
     fine = grids[1]
@@ -574,7 +578,7 @@
                     for odd in range(2):
                         raised[1][g, member, t, pl.ds(2 * start + odd, SUB, stride=2), :] = part
     (a0, z0), (a1, z1) = level_rows
-    add_raised(fine, u[1], raised[1], 0, fine.rows // SUB)
+    add_raised(fine, old[1], u[1], raised[1], a1 - 1, z1 + 1)
     relax_strips(fine, ends, u[1], f[1], d[1], a1, z1)
 
     for group in range(fine.groups):
@@ -586,11 +590,12 @@
                     part = u[1][group, member, tile, rows, :] - uc[1][group, member, tile, rows, :]
                     for odd in range(2):
                         raised[0][group, member, tile, pl.ds(2 * start + odd, SUB, stride=2), :] = part
-    add_raised(grids[0], u[0], raised[0], 2 * a1, 2 * z1)
+    span = max(2 * a1, a0 - 1), min(2 * z1, z0 + 1)
+    add_raised(grids[0], old[0], u[0], raised[0], *span)
     relax_strips(grids[0], ends, u[0], f[0], d[0], a0, z0)
 
 
-def add_raised(grid, field, raised, first, last):
+def add_raised(grid, before, field, raised, first, last):
     period = grid.tiles // 2 if grid.split else grid.tiles
     for group in range(grid.groups):
         for member in range(2):
@@ -598,7 +603,7 @@
                 for strip in range(first, last):
                     rows = pl.ds(strip * SUB, SUB)
                     field[group, member, tile, rows, :] = (
-                        field[group, member, tile, rows, :]
+                        before[group, member, tile, rows, :]
                         + raised[group, member, tile % period, rows, :]
                     )
 
@@ -740,12 +745,11 @@
 ):
     grids = sizes.grids
     row_index, ends = domain_ends(sizes)
-    for source, target in ((u0i, u0), (u1i, u1), (u2i, u2)):
-        target[...] = source[...]
     scratch = (correction, (raised0, raised1, raised2))
     fields = [(received, k, 3) for k in range(3)]
     span = middle_rows(sizes)
-    state = ((u0, u1, u2), (f0, f1i, f2i), (d0, d1, d2), (None, uc1i, uc2i))
+    old = (u0i, u1i, u2i)
+    state = (old, (u0, u1, u2), (f0, f1i, f2i), (d0, d1, d2), (None, uc1i, uc2i))
     ascend(sizes, ends, row_index, mixing, fields, state, scratch, span)
     (a0, z0), _ = span
     relax_strips(grids[0], ends, u0, f0, d0, a0, z0)
@@ -762,13 +766,12 @@
 ):
     grids = sizes.grids
     row_index, ends = domain_ends(sizes)
-    for source, target in ((u0, v0), (u1, v1), (u2, v2)):
-        target[...] = source[...]
     scratch = (correction, (raised0, raised1, raised2))
     fields = [(received, 0, 2), (received, 1, 2), (first_received, 2, 3)]
     own = (sizes.rows // SUB, 2 * sizes.rows // SUB)
     span = (own, middle_rows(sizes)[1])
-    state = ((v0, v1, v2), (f0, f1, f2), (d0, d1, d2), (None, uc1, uc2))
+    old = (u0, u1, u2)
+    state = (old, (v0, v1, v2), (f0, f1, f2), (d0, d1, d2), (None, uc1, uc2))
     ascend(sizes, ends, row_index, mixing, fields, state, scratch, span)
     column_index = lax.axis_index("gy")
     lane = lane_of()

time: 43.1 us -> 43 us (level)
  no operation moved by 1% of the time
where the time goes in v5:
time: 43 us; the launch traced here: 42.7 us
  blocking collectives  25.9 us (60%)
  Pallas kernels  7.61 us (18%)
  waiting for transfers between devices  3.89 us (9%)
  starting transfers between devices  3.76 us (9%)
  other arithmetic  0.82 us (2%)
  local copies, waits for them, and re-layouts  0.72 us (2%)
    all_to_all x2, blocking collectives, local(): lax.all_to_all(message, ('gx', 'gy'), 0, 0, tiled=True).reshape(-1, LANES)  25.9 us
    ppermute x2, starting transfers between devices, local(): beside = [lax.ppermute(raw, 'gx', far), lax.ppermute(raw, 'gx', near)][::-1]  3.69 us
    pallas_call x1, Pallas kernels, local(): call(middle_kernel, outs, coarse + rests)  3.36 us
    ppermute x2, waiting for transfers between devices, local(): beside = [lax.ppermute(raw, 'gx', far), lax.ppermute(raw, 'gx', near)][::-1]  2.83 us
    pallas_call x1, Pallas kernels, local(): call(last_kernel, outs, [vmem(shape) for shape in fields] + coarse)  2.66 us
    pallas_call x1, Pallas kernels, local(): call(start_kernel, outs, [vmem((sizes.tiles,) + tiles.shape[:3] + (2 * LA...  1.58 us
    ppermute x1, waiting for transfers between devices, local(): pieces = (tiles, lax.ppermute(tiles, 'gy', [(0, 1), (1, 0)]))  1.06 us
  transfers between devices with their start and end apart: 3, of which 2 were waited for; matrix products, arithmetic and copies ran while one was open for 0% of the time, Pallas kernels for 0%

profile of v5, /device:TPU:0, one launch (start us, length us, event | category | flops | bytes accessed | tf_op | source)
XLA Modules:
  0.0 42.7 jit_solution(5954339963518472226)
XLA Ops:
  0.0 0.8 %fusion = (f32[1,8,32,128]{3,2,1,0:T(8,128)S(1)}, f32[8,32,128]{2,1,0:T(8,128)S(1)}) fusion(bf16[4,32,128]{2,1,0:T(8,128)(2,1)} %bitcast.13, bf16[4,32,128]{2,1,0:T(8,128)(2,1)} %bitcast.14), kind=kLoop, calls=%fused_computation.2 | loop fusion | flops 65536 | bytes 327680 | tf_op jit(solution)/shard_map/stack | solution.py:813
  0.8 3.0 %collective-permute-start = (f32[8,32,128]{2,1,0:T(8,128)S(1)}, f32[8,32,128]{2,1,0:T(8,128)S(1)}, u32[]{:S(2)}, u32[]{:S(2)}) collective-permute-start(f32[8,32,128]{2,1,0:T(8,128)S(1)} %get-tuple-element.46), channel_id=1, source_target_pairs={{0,2},{2,0},{4,6},{6,4},{8,10},{10,8},{12,14},{14,12},{16,18},{18,... | collective-permute-start | bytes 393224 | tf_op jit(solution)/shard_map/ppermute | solution.py:812
  3.8 0.7 %collective-permute-start.1 = (f32[8,32,128]{2,1,0:T(8,128)S(1)}, f32[8,32,128]{2,1,0:T(8,128)S(1)}, u32[]{:S(2)}, u32[]{:S(2)}) collective-permute-start(f32[8,32,128]{2,1,0:T(8,128)S(1)} %get-tuple-element.46), channel_id=1, source_target_pairs={{2,4},{4,2},{6,8},{8,6},{10,12},{12,10},{14,16},{16,14},{18,20},{2... | collective-permute-start | bytes 393224 | tf_op jit(solution)/shard_map/ppermute | solution.py:812
  4.5 2.8 %collective-permute-done = f32[8,32,128]{2,1,0:T(8,128)S(1)} collective-permute-done((f32[8,32,128]{2,1,0:T(8,128)S(1)}, f32[8,32,128]{2,1,0:T(8,128)S(1)}, u32[]{:S(2)}, u32[]{:S(2)}) %collective-permute-start) | collective-permute-done | bytes 131104 | tf_op jit(solution)/shard_map/ppermute | solution.py:812
  7.3 0.0 collective-permute-done.1
  7.3 0.0 copy-start
  7.4 0.1 collective-permute-start.2
  7.4 0.6 %copy-done = f32[2,2]{1,0:T(2,128)S(1)} copy-done((f32[2,2]{1,0:T(2,128)S(1)}, f32[2,2]{1,0:T(2,128)}, u32[]{:S(2)}) %copy-start) | copy-done | bytes 40
  8.0 0.1 broadcast_in_dim.7
  8.1 1.1 %collective-permute-done.2.refs_2_ = f32[3,8,32,128]{3,2,1,0:T(8,128)S(1)} collective-permute-done((f32[3,8,32,128]{3,2,1,0:T(8,128)S(1)}, f32[3,8,32,128]{3,2,1,0:T(8,128)S(1)}, u32[]{:S(2)}, u32[]{:S(2)}) %collective-permute-start.2) | collective-permute-done | bytes 393248 | tf_op jit(solution)/shard_map/ppermute | solution.py:815
  9.2 0.1 broadcast_in_dim.8.refs_0_
  9.2 1.6 %start_kernel.1 = (f32[2,2,2,104,128]{4,3,2,1,0:T(8,128)S(1)}, f32[2,2,1,56,128]{4,3,2,1,0:T(8,128)S(1)}, f32[1,2,1,32,128]{4,3,2,1,0:T(8,128)S(1)}, f32[2,2,2,1...) custom-call(f32[4,8,128]{2,1,0:T(8,128)S(1)} %broadcast_in_dim.8.ref, ...), custom_call_target="tpu_custom_call" | custom-call | tf_op jit(solution)/shard_map/start_kernel/pallas_call | solution.py:862
  10.8 16.8 %all_to_all.10 = f32[32,3,2,128]{3,2,1,0:T(2,128)S(1)} all-to-all(f32[32,3,2,128]{3,2,1,0:T(2,128)S(1)} %get-tuple-element.25), channel_id=1, replica_groups=mesh['gx'=16,'gy'=2] {'gx','gy'}, dimensions={0} | all-to-all | bytes 196608 | tf_op jit(solution)/shard_map/all_to_all | solution.py:865
  27.6 3.4 %middle_kernel.1 = (f32[2,2,2,104,128]{4,3,2,1,0:T(8,128)S(1)}, f32[2,2,1,56,128]{4,3,2,1,0:T(8,128)S(1)}, f32[1,2,1,32,128]{4,3,2,1,0:T(8,128)S(1)}, f32[2,2,1,...) custom-call(f32[4,8,128]{2,1,0:T(8,128)S(1)} %broadcast_in_dim.8.ref, ...), custom_call_target="tpu_custom_call" | custom-call | tf_op jit(solution)/shard_map/middle_kernel/pallas_call | solution.py:867
  30.9 9.1 %all_to_all.11 = f32[32,1,4,128]{3,2,1,0:T(4,128)S(1)} all-to-all(f32[32,1,4,128]{3,2,1,0:T(4,128)S(1)} %get-tuple-element.37), channel_id=1, replica_groups=mesh['gx'=16,'gy'=2] {'gx','gy'}, dimensions={0} | all-to-all | bytes 131072 | tf_op jit(solution)/shard_map/all_to_all | solution.py:870
  40.1 2.7 %last_kernel.1 = f32[2,2,32,128]{3,2,1,0:T(8,128)} custom-call(f32[4,8,128]{2,1,0:T(8,128)S(1)} %broadcast_in_dim.8.refs_0_, f32[128,128]{1,0:T(8,128)S(1)} %bitcast.10, f32[192,128]{1,0:T(8,128)S(1)} %bitcast.9, f32[2,2,2,104,128]{4,3,2,1,0:T(8,128)S(1)} %get-tuple-element.38.refs_3_, f32[2,2,1,56,128]{4,3,2,1,0:T(8,128)S(1)} %get-tuple-element.39.refs_4_, ...), custom_call_target="tpu_custom_call" | custom-call | tf_op jit(solution)/shard_map/last_kernel/pallas_call | solution.py:872
  (1 shorter events, 0.0 us)
Async XLA Ops:
  0.8 6.5 %collective-permute-start = (f32[8,32,128]{2,1,0:T(8,128)S(1)}, f32[8,32,128]{2,1,0:T(8,128)S(1)}, u32[]{:S(2)}, u32[]{:S(2)}) collective-permute-start(f32[8,32,128]{2,1,0:T(8,128)S(1)} %get-tuple-element.46), channel_id=1, source_target_pairs={{0,2},{2,0},{4,6},{6,4},{8,10},{10,8},{12,14},{14,12},{16,18},{18,... | collective-permute-start | bytes 393224 | tf_op jit(solution)/shard_map/ppermute | solution.py:812
  3.8 3.5 %collective-permute-start.1 = (f32[8,32,128]{2,1,0:T(8,128)S(1)}, f32[8,32,128]{2,1,0:T(8,128)S(1)}, u32[]{:S(2)}, u32[]{:S(2)}) collective-permute-start(f32[8,32,128]{2,1,0:T(8,128)S(1)} %get-tuple-element.46), channel_id=1, source_target_pairs={{2,4},{4,2},{6,8},{8,6},{10,12},{12,10},{14,16},{16,14},{18,20},{2... | collective-permute-start | bytes 393224 | tf_op jit(solution)/shard_map/ppermute | solution.py:812
  7.3 0.7 %copy-start = (f32[2,2]{1,0:T(2,128)S(1)}, f32[2,2]{1,0:T(2,128)}, u32[]{:S(2)}) copy-start(f32[2,2]{1,0:T(2,128)} %param.5) | copy-start | bytes 52
  7.4 1.8 %collective-permute-start.2 = (f32[3,8,32,128]{3,2,1,0:T(8,128)S(1)}, f32[3,8,32,128]{3,2,1,0:T(8,128)S(1)}, u32[]{:S(2)}, u32[]{:S(2)}) collective-permute-start(f32[3,8,32,128]{3,2,1,0:T(8,128)S(1)} %pad_maximum_fusion.refs_1_), channel_id=1, source_target_pairs={{0,1},{1,0},{2,3},{3,2},{4,5},{5,4},{6,7},{7,6},{8,9},{9,8},{10,11... | collective-permute-start | bytes 1179656 | tf_op jit(solution)/shard_map/ppermute | solution.py:815

commit v6 on v5

--- a/solution.py
+++ b/solution.py
@@ -638,7 +638,7 @@
     select = (source == wanted).astype(jnp.float32).astype(jnp.bfloat16)
     for tile in range(sizes.tiles):
         for part in range(3):
-            sides = [piece[part] for piece in pieces[2 * tile : 2 * tile + 2]]
+            sides = [piece[part][...] for piece in pieces[2 * tile : 2 * tile + 2]]
             sides = [side.reshape(-1, LANES).astype(jnp.bfloat16) for side in sides]
             both = jnp.concatenate(sides, axis=1)
             result = jnp.dot(both, select, preferred_element_type=jnp.float32)
@@ -647,10 +647,17 @@
 
 def start_kernel(sizes, mixing, *refs):
     if sizes.column_devices == 2:
-        pieces, refs = refs[:2], refs[2:]
+        mine, early, late, *refs = refs
+        pieces = [
+            [mine.at[part] for part in range(3)],
+            [early.at[0], early.at[1], late],
+        ]
         swapped = lax.axis_index("gy")
     else:
-        pieces, refs = [refs[0].at[k] for k in range(sizes.column_devices)], refs[1:]
+        pieces = [
+            [refs[0].at[k, part] for part in range(3)] for k in range(sizes.column_devices)
+        ]
+        refs = refs[1:]
         swapped = 0
     u0, u1, u2, f0, f1, f2, d0, d1, d2, uc1, uc2, message, ordered, w0, w1, w2, *rest = refs
     split_columns(sizes, pieces, swapped, ordered)
@@ -812,7 +819,8 @@
     beside = [lax.ppermute(raw, "gx", far), lax.ppermute(raw, "gx", near)][::-1]
     tiles = jnp.stack([raw] + beside)
     if column_devices == 2:
-        pieces = (tiles, lax.ppermute(tiles, "gy", [(0, 1), (1, 0)]))
+        swap = lambda value: lax.ppermute(value, "gy", [(0, 1), (1, 0)])
+        pieces = (tiles, swap(jnp.stack([raw, beside[0]])), swap(beside[1]))
     else:
         pieces = (lax.all_gather(tiles, "gy"),)
 

time: 43 us -> 42.5 us (0.988)
  blocking collectives: 25.9 us -> 25.4 us
  starting transfers between devices: 3.76 us -> 4.25 us
  local copies, waits for them, and re-layouts: 0.72 us -> 0.23 us
    unnamed x2, local copies, waits for them, and re-layouts: 0.57 us -> 0.08 us
    ppermute x1 -> x2, starting transfers between devices: 0.07 us -> 0.56 us  [local(): swap = lambda value: lax.ppermute(value, 'gy', [(0, 1), (1, 0)])]
    all_to_all x2, blocking collectives: 25.9 us -> 25.4 us  [local(): lax.all_to_all(message, ('gx', 'gy'), 0, 0, tiled=True).reshape(-1, LANES)]
    ppermute x1 -> x2, waiting for transfers between devices: 1.06 us -> 1.02 us  [local(): swap = lambda value: lax.ppermute(value, 'gy', [(0, 1), (1, 0)])]
  transfers between devices with their start and end apart: 3 -> 4, of which waited for: 2 -> 2; matrix products, arithmetic and copies ran while one was open for 0% -> 0% of each run, Pallas kernels for 0% -> 0%
where the time goes in v6:
time: 42.5 us; the launch traced here: 42.2 us
  blocking collectives  25.4 us (60%)
  Pallas kernels  7.61 us (18%)
  starting transfers between devices  4.25 us (10%)
  waiting for transfers between devices  3.86 us (9%)
  other arithmetic  0.84 us (2%)
    all_to_all x2, blocking collectives, local(): lax.all_to_all(message, ('gx', 'gy'), 0, 0, tiled=True).reshape(-1, LANES)  25.4 us
    ppermute x2, starting transfers between devices, local(): beside = [lax.ppermute(raw, 'gx', far), lax.ppermute(raw, 'gx', near)][::-1]  3.69 us
    pallas_call x1, Pallas kernels, local(): call(middle_kernel, outs, coarse + rests)  3.36 us
    ppermute x2, waiting for transfers between devices, local(): beside = [lax.ppermute(raw, 'gx', far), lax.ppermute(raw, 'gx', near)][::-1]  2.83 us
    pallas_call x1, Pallas kernels, local(): call(last_kernel, outs, [vmem(shape) for shape in fields] + coarse)  2.66 us
    pallas_call x1, Pallas kernels, local(): call(start_kernel, outs, [vmem((sizes.tiles,) + tiles.shape[:3] + (2 * LA...  1.58 us
    ppermute x2, waiting for transfers between devices, local(): swap = lambda value: lax.ppermute(value, 'gy', [(0, 1), (1, 0)])  1.02 us
  transfers between devices with their start and end apart: 4, of which 2 were waited for; matrix products, arithmetic and copies ran while one was open for 0% of the time, Pallas kernels for 0%

profile of v6, /device:TPU:0, one launch (start us, length us, event | category | flops | bytes accessed | tf_op | source)
XLA Modules:
  0.0 42.2 jit_solution(581326068667861285)
XLA Ops:
  0.0 0.8 %fusion = (f32[1,8,32,128]{3,2,1,0:T(8,128)S(1)}, f32[8,32,128]{2,1,0:T(8,128)S(1)}) fusion(bf16[4,32,128]{2,1,0:T(8,128)(2,1)} %bitcast.14, bf16[4,32,128]{2,1,0:T(8,128)(2,1)} %bitcast.15), kind=kLoop, calls=%fused_computation.3 | loop fusion | flops 65536 | bytes 327680 | tf_op jit(solution)/shard_map/stack | solution.py:820
  0.8 3.0 %collective-permute-start = (f32[8,32,128]{2,1,0:T(8,128)S(1)}, f32[8,32,128]{2,1,0:T(8,128)S(1)}, u32[]{:S(2)}, u32[]{:S(2)}) collective-permute-start(f32[8,32,128]{2,1,0:T(8,128)S(1)} %get-tuple-element.46), channel_id=1, source_target_pairs={{0,2},{2,0},{4,6},{6,4},{8,10},{10,8},{12,14},{14,12},{16,18},{18,... | collective-permute-start | bytes 393224 | tf_op jit(solution)/shard_map/ppermute | solution.py:819
  3.8 0.7 %collective-permute-start.1 = (f32[8,32,128]{2,1,0:T(8,128)S(1)}, f32[8,32,128]{2,1,0:T(8,128)S(1)}, u32[]{:S(2)}, u32[]{:S(2)}) collective-permute-start(f32[8,32,128]{2,1,0:T(8,128)S(1)} %get-tuple-element.46), channel_id=1, source_target_pairs={{2,4},{4,2},{6,8},{8,6},{10,12},{12,10},{14,16},{16,14},{18,20},{2... | collective-permute-start | bytes 393224 | tf_op jit(solution)/shard_map/ppermute | solution.py:819
  4.5 2.8 %collective-permute-done = f32[8,32,128]{2,1,0:T(8,128)S(1)} collective-permute-done((f32[8,32,128]{2,1,0:T(8,128)S(1)}, f32[8,32,128]{2,1,0:T(8,128)S(1)}, u32[]{:S(2)}, u32[]{:S(2)}) %collective-permute-start) | collective-permute-done | bytes 131104 | tf_op jit(solution)/shard_map/ppermute | solution.py:819
  7.3 0.0 copy-start
  7.4 0.1 collective-permute-start.2
  7.4 0.0 collective-permute-done.1
  7.4 0.5 %collective-permute-start.3 = (f32[8,32,128]{2,1,0:T(8,128)S(1)}, f32[8,32,128]{2,1,0:T(8,128)S(1)}, u32[]{:S(2)}, u32[]{:S(2)}) collective-permute-start(f32[8,32,128]{2,1,0:T(8,128)S(1)} %collective-permute-done.1), channel_id=1, source_target_pairs={{0,1},{1,0},{2,3},{3,2},{4,5},{5,4},{6,7},{7,6},{8,9},{9,8},{10,11... | collective-permute-start | bytes 393224 | tf_op jit(solution)/shard_map/ppermute | solution.py:822
  7.9 0.1 copy-done
  8.0 0.1 broadcast_in_dim.7
  8.1 1.0 %collective-permute-done.3.refs_3_ = f32[8,32,128]{2,1,0:T(8,128)S(1)} collective-permute-done((f32[8,32,128]{2,1,0:T(8,128)S(1)}, f32[8,32,128]{2,1,0:T(8,128)S(1)}, u32[]{:S(2)}, u32[]{:S(2)}) %collective-permute-start.3) | collective-permute-done | bytes 131104 | tf_op jit(solution)/shard_map/ppermute | solution.py:822
  9.1 0.0 collective-permute-done.2.refs_2_
  9.1 0.1 broadcast_in_dim.8.refs_0_
  9.2 1.6 %start_kernel.1 = (f32[2,2,2,104,128]{4,3,2,1,0:T(8,128)S(1)}, f32[2,2,1,56,128]{4,3,2,1,0:T(8,128)S(1)}, f32[1,2,1,32,128]{4,3,2,1,0:T(8,128)S(1)}, f32[2,2,2,1...) custom-call(f32[4,8,128]{2,1,0:T(8,128)S(1)} %broadcast_in_dim.8.ref, ...), custom_call_target="tpu_custom_call" | custom-call | tf_op jit(solution)/shard_map/start_kernel/pallas_call | solution.py:870
  10.8 16.3 %all_to_all.10 = f32[32,3,2,128]{3,2,1,0:T(2,128)S(1)} all-to-all(f32[32,3,2,128]{3,2,1,0:T(2,128)S(1)} %get-tuple-element.25), channel_id=1, replica_groups=mesh['gx'=16,'gy'=2] {'gx','gy'}, dimensions={0} | all-to-all | bytes 196608 | tf_op jit(solution)/shard_map/all_to_all | solution.py:873
  27.1 3.4 %middle_kernel.1 = (f32[2,2,2,104,128]{4,3,2,1,0:T(8,128)S(1)}, f32[2,2,1,56,128]{4,3,2,1,0:T(8,128)S(1)}, f32[1,2,1,32,128]{4,3,2,1,0:T(8,128)S(1)}, f32[2,2,1,...) custom-call(f32[4,8,128]{2,1,0:T(8,128)S(1)} %broadcast_in_dim.8.ref, ...), custom_call_target="tpu_custom_call" | custom-call | tf_op jit(solution)/shard_map/middle_kernel/pallas_call | solution.py:875
  30.5 9.1 %all_to_all.11 = f32[32,1,4,128]{3,2,1,0:T(4,128)S(1)} all-to-all(f32[32,1,4,128]{3,2,1,0:T(4,128)S(1)} %get-tuple-element.37), channel_id=1, replica_groups=mesh['gx'=16,'gy'=2] {'gx','gy'}, dimensions={0} | all-to-all | bytes 131072 | tf_op jit(solution)/shard_map/all_to_all | solution.py:878
  39.6 2.7 %last_kernel.1 = f32[2,2,32,128]{3,2,1,0:T(8,128)} custom-call(f32[4,8,128]{2,1,0:T(8,128)S(1)} %broadcast_in_dim.8.refs_0_, f32[128,128]{1,0:T(8,128)S(1)} %bitcast.10, f32[192,128]{1,0:T(8,128)S(1)} %bitcast.9, f32[2,2,2,104,128]{4,3,2,1,0:T(8,128)S(1)} %get-tuple-element.38.refs_3_, f32[2,2,1,56,128]{4,3,2,1,0:T(8,128)S(1)} %get-tuple-element.39.refs_4_, ...), custom_call_target="tpu_custom_call" | custom-call | tf_op jit(solution)/shard_map/last_kernel/pallas_call | solution.py:880
  (2 shorter events, 0.0 us)
Async XLA Ops:
  0.8 6.5 %collective-permute-start = (f32[8,32,128]{2,1,0:T(8,128)S(1)}, f32[8,32,128]{2,1,0:T(8,128)S(1)}, u32[]{:S(2)}, u32[]{:S(2)}) collective-permute-start(f32[8,32,128]{2,1,0:T(8,128)S(1)} %get-tuple-element.46), channel_id=1, source_target_pairs={{0,2},{2,0},{4,6},{6,4},{8,10},{10,8},{12,14},{14,12},{16,18},{18,... | collective-permute-start | bytes 393224 | tf_op jit(solution)/shard_map/ppermute | solution.py:819
  3.8 3.6 %collective-permute-start.1 = (f32[8,32,128]{2,1,0:T(8,128)S(1)}, f32[8,32,128]{2,1,0:T(8,128)S(1)}, u32[]{:S(2)}, u32[]{:S(2)}) collective-permute-start(f32[8,32,128]{2,1,0:T(8,128)S(1)} %get-tuple-element.46), channel_id=1, source_target_pairs={{2,4},{4,2},{6,8},{8,6},{10,12},{12,10},{14,16},{16,14},{18,20},{2... | collective-permute-start | bytes 393224 | tf_op jit(solution)/shard_map/ppermute | solution.py:819
  7.3 0.7 %copy-start = (f32[2,2]{1,0:T(2,128)S(1)}, f32[2,2]{1,0:T(2,128)}, u32[]{:S(2)}) copy-start(f32[2,2]{1,0:T(2,128)} %param.5) | copy-start | bytes 52
  7.4 1.8 %collective-permute-start.2 = (f32[2,8,32,128]{3,2,1,0:T(8,128)S(1)}, f32[2,8,32,128]{3,2,1,0:T(8,128)S(1)}, u32[]{:S(2)}, u32[]{:S(2)}) collective-permute-start(f32[2,8,32,128]{3,2,1,0:T(8,128)S(1)} %pad_maximum_fusion.1), channel_id=1, source_target_pairs={{0,1},{1,0},{2,3},{3,2},{4,5},{5,4},{6,7},{7,6},{8,9},{9,8},{10,11... | collective-permute-start | bytes 786440 | tf_op jit(solution)/shard_map/ppermute | solution.py:822
  7.4 1.7 %collective-permute-start.3 = (f32[8,32,128]{2,1,0:T(8,128)S(1)}, f32[8,32,128]{2,1,0:T(8,128)S(1)}, u32[]{:S(2)}, u32[]{:S(2)}) collective-permute-start(f32[8,32,128]{2,1,0:T(8,128)S(1)} %collective-permute-done.1), channel_id=1, source_target_pairs={{0,1},{1,0},{2,3},{3,2},{4,5},{5,4},{6,7},{7,6},{8,9},{9,8},{10,11... | collective-permute-start | bytes 393224 | tf_op jit(solution)/shard_map/ppermute | solution.py:822
